TPU v7x, 256 devices: a whole 4x4x8 slice. The times are simulated.
256 devices in a mesh: seq: 16 (over x, z_hi, core), chan: 16 (over z_lo, y).
Axes of the slice: x: 4, y: 4, z: 8 (z_hi: 2, z_lo: 4; z = z_hi * 4 + z_lo), core: 2. Of those that a mesh axis runs over, the one named last changes fastest.
Arguments:
- values: bfloat16 [1024, 16384], P('chan', 'seq'), may hold values from -6 to 6
- gate_acts: bfloat16 [1024, 16384], P('chan', 'seq'), may hold values from -6 to 6
- cotangent: bfloat16 [1024, 16384], P('chan', 'seq'), may hold values from -6 to 6
- filter_taps: float32 [1024, 16384], P('chan', 'seq'), may hold values from -160 to 160
- w_value: bfloat16 [1024, 1024], replicated, may hold values from -0.1875 to 0.1875
- w_gate: bfloat16 [1024, 1024], replicated, may hold values from -0.1875 to 0.1875
Outputs:
- input_grad: bfloat16 [16384, 1024], P(('seq', 'chan'))
- filter_grad: float32 [1024, 16384], P('chan', 'seq')
All inputs are finite; a program needn't handle non-finite values.
Results may differ from a plain program's by a relative error of at most 0.005.
Values may be sent and summed in bfloat16 or wider, within the bound.
A program may use at most 64 MiB of HBM per device.

v0:
```python
import math

import jax
import jax.numpy as jnp
from jax import lax
from jax.sharding import PartitionSpec as P

exact_mode = lax.Precision.HIGHEST


def from_partner(block, axis, apart):
    count = lax.axis_size(axis)
    route = []
    for low in range(count):
        high = low | 1 << apart
        if high != low and high < count:
            route += [(low, high), (high, low)]
    return lax.ppermute(block, axis, route)


def complex_times(left_re, left_im, right_re, right_im):
    return (left_re * right_re - left_im * right_im, left_re * right_im + left_im * right_re)


def dft_tables(seq_len):
    ladder = jnp.arange(seq_len, dtype=jnp.int32)
    product = ladder[:, None] * ladder[None, :] % seq_len
    angle = product.astype(jnp.float32) * (2.0 * math.pi / seq_len)
    return (jnp.cos(angle), jnp.sin(angle))


def local_dft(stacked, tables, inverse):
    cos_tab, sin_tab = tables
    rows = stacked.shape[1]
    seq_len = stacked.shape[2]
    flat = stacked.reshape(2 * rows, seq_len)
    first = jnp.dot(flat, cos_tab, precision=exact_mode).reshape(2, rows, seq_len)
    second = jnp.dot(flat, sin_tab, precision=exact_mode).reshape(2, rows, seq_len)
    if inverse:
        real_part = (first[0] - second[1]) / seq_len
        imag_part = (first[1] + second[0]) / seq_len
    else:
        real_part = first[0] + second[1]
        imag_part = first[1] - second[0]
    return jnp.stack([real_part, imag_part])


def pair_twiddle(my_index, bit_level, seq_len):
    stride = 2**bit_level
    within = my_index % stride * seq_len + jnp.arange(seq_len, dtype=jnp.int32)
    angle = within.astype(jnp.float32) * (math.pi / (seq_len * stride))
    high_side = my_index // stride % 2
    return (jnp.cos(angle), -jnp.sin(angle), high_side)


def partner(stacked, bit_level):
    return from_partner(stacked, "seq", bit_level)


def forward_pairs(stacked, tables, my_index, n_seq):
    seq_len = stacked.shape[2]
    for bit_level in reversed(range(n_seq.bit_length() - 1)):
        tw_re, tw_im, high_side = pair_twiddle(my_index, bit_level, seq_len)
        is_high = high_side == 1
        sign = (1 - 2 * high_side).astype(jnp.float32)
        other = partner(stacked, bit_level)
        mixed = other + sign * stacked
        w_re = jnp.where(is_high, tw_re, 1.0)
        w_im = jnp.where(is_high, tw_im, 0.0)
        real_part, imag_part = complex_times(mixed[0], mixed[1], w_re, w_im)
        stacked = jnp.stack([real_part, imag_part])
    return local_dft(stacked, tables, False)


def inverse_pairs(stacked, tables, my_index, n_seq):
    seq_len = stacked.shape[2]
    stacked = local_dft(stacked, tables, True)
    for bit_level in range(n_seq.bit_length() - 1):
        tw_re, tw_im, high_side = pair_twiddle(my_index, bit_level, seq_len)
        is_high = high_side == 1
        sign = (1 - 2 * high_side).astype(jnp.float32)
        w_re = jnp.where(is_high, tw_re, 1.0)
        w_im = jnp.where(is_high, -tw_im, 0.0)
        real_part, imag_part = complex_times(stacked[0], stacked[1], w_re, w_im)
        turned = jnp.stack([real_part, imag_part])
        other = partner(turned, bit_level)
        stacked = 0.5 * (other + sign * turned)
    return stacked


def spread_grads(values, gate_acts, cotangent, filter_taps, n_seq, my_index):
    channels = values.shape[0]
    seq_len = values.shape[1]
    total = seq_len * n_seq
    factor = 1.0 / math.sqrt(total)
    tables = dft_tables(seq_len)
    positions = my_index * seq_len + jnp.arange(seq_len, dtype=jnp.int32)
    angle = positions.astype(jnp.float32) * (math.pi / total)
    shift_re = jnp.cos(angle)
    shift_im = -jnp.sin(angle)
    upstream = cotangent.astype(jnp.float32) * gate_acts.astype(jnp.float32)
    base = jnp.concatenate([filter_taps * factor, values.astype(jnp.float32), upstream], 0)
    stacked = jnp.stack(
        [
            jnp.concatenate([base, base * shift_re], 0),
            jnp.concatenate([jnp.zeros_like(base), base * shift_im], 0),
        ]
    )
    spectra = forward_pairs(stacked, tables, my_index, n_seq)

    def section(index):
        return (
            spectra[0, index * channels : (index + 1) * channels],
            spectra[1, index * channels : (index + 1) * channels],
        )

    real_rows = []
    imag_rows = []
    for half_start in (0, 3):
        kern_re, kern_im = section(half_start)
        sig_re, sig_im = section(half_start + 1)
        grad_re, grad_im = section(half_start + 2)
        conv_re, conv_im = complex_times(kern_re, kern_im, sig_re, sig_im)
        vgrad_re, vgrad_im = complex_times(kern_re, -kern_im, grad_re, grad_im)
        tgrad_re, tgrad_im = complex_times(grad_re, grad_im, sig_re, -sig_im)
        real_rows = real_rows + [conv_re, vgrad_re, tgrad_re]
        imag_rows = imag_rows + [conv_im, vgrad_im, tgrad_im]
    products = jnp.stack([jnp.concatenate(real_rows, 0), jnp.concatenate(imag_rows, 0)])
    signals = inverse_pairs(products, tables, my_index, n_seq)
    width3 = 3 * channels
    merged = 0.5 * (
        signals[0, :width3] + shift_re * signals[0, width3:] + shift_im * signals[1, width3:]
    )
    conv_out = merged[:channels]
    value_grad = merged[channels : 2 * channels].astype(jnp.bfloat16)
    taps_grad = merged[2 * channels :] * factor
    gate_grad = (cotangent.astype(jnp.float32) * conv_out).astype(jnp.bfloat16)
    return (value_grad, gate_grad, taps_grad)


def local(values, gate_acts, cotangent, filter_taps, w_value, w_gate):
    n_seq = lax.axis_size("seq")
    my_index = lax.axis_index("seq")
    value_grad, gate_grad, taps_grad = spread_grads(
        values, gate_acts, cotangent, filter_taps, n_seq, my_index
    )
    got_value, got_gate = (
        lax.all_to_all(value_grad, "chan", split_axis=1, concat_axis=0, tiled=True),
        lax.all_to_all(gate_grad, "chan", split_axis=1, concat_axis=0, tiled=True),
    )
    contract = (((0,), (1,)), ((), ()))
    input_grad = lax.dot_general(got_value, w_value, contract, preferred_element_type=jnp.float32)
    input_grad = input_grad + lax.dot_general(
        got_gate, w_gate, contract, preferred_element_type=jnp.float32
    )
    return (input_grad.astype(jnp.bfloat16), taps_grad)


def solution(mesh):
    return jax.shard_map(
        local,
        mesh=mesh,
        in_specs=(P("chan", "seq"), P("chan", "seq"), P("chan", "seq"), P("chan", "seq"), P(), P()),
        out_specs=(P(("seq", "chan"), None), P("chan", "seq")),
        check_vma=False,
    )
```

profile of v0, /device:TPU:1, one launch (start us, length us, event | category | flops | bytes accessed | tf_op | source)
XLA Modules:
  0.0 757.7 jit_solution(8698564870906739941)
XLA Ops:
  0.7 1.1 convert_element_type.112
  1.8 1.1 convert_multiply_fusion.1
  3.5 2.2 pad_maximum_fusion
  5.9 3.6 collective-permute-start
  9.6 67.1 %collective-permute-done = f32[2,384,1024]{2,1,0:T(8,128)} collective-permute-done((f32[2,384,1024]{2,1,0:T(8,128)}, f32[2,384,1024]{2,1,0:T(8,128)}, u32[]{:S(2)}, u32[]{:S(2)}) %collective-permute-start) | collective-permute-done | bytes 3145760 | tf_op jit(solution)/shard_map/ppermute | solution.py:18
  76.6 3.8 multiply_add_fusion.3
  80.9 2.1 pad_maximum_fusion.1
  83.5 2.2 collective-permute-start.1
  85.8 66.9 %collective-permute-done.1 = f32[2,384,1024]{2,1,0:T(8,128)} collective-permute-done((f32[2,384,1024]{2,1,0:T(8,128)}, f32[2,384,1024]{2,1,0:T(8,128)}, u32[]{:S(2)}, u32[]{:S(2)}) %collective-permute-start.1) | collective-permute-done | bytes 3145760 | tf_op jit(solution)/shard_map/ppermute | solution.py:18
  152.7 3.8 multiply_add_fusion.2
  157.0 2.1 pad_maximum_fusion.2
  159.6 7.2 collective-permute-start.2
  166.8 98.4 %collective-permute-done.2 = f32[2,384,1024]{2,1,0:T(8,128)} collective-permute-done((f32[2,384,1024]{2,1,0:T(8,128)}, f32[2,384,1024]{2,1,0:T(8,128)}, u32[]{:S(2)}, u32[]{:S(2)}) %collective-permute-start.2) | collective-permute-done | bytes 3145760 | tf_op jit(solution)/shard_map/ppermute | solution.py:18
  265.2 3.8 multiply_add_fusion.1
  269.5 2.1 pad_maximum_fusion.3
  272.2 38.0 %collective-permute-start.3 = (f32[2,384,1024]{2,1,0:T(8,128)}, f32[2,384,1024]{2,1,0:T(8,128)}, u32[]{:S(2)}, u32[]{:S(2)}) collective-permute-start(f32[2,384,1024]{2,1,0:T(8,128)} %pad_maximum_fusion.3), channel_id=1, source_target_pairs={{0,16},{16,0},{32,48},{48,32},{64,80},{80,64},{96,112},{112,96},{1... | collective-permute-start | bytes 9437192 | tf_op jit(solution)/shard_map/ppermute | solution.py:18
  310.3 5.5 collective-permute-done.3
  315.8 3.8 multiply_add_fusion
  320.5 26.9 %fusion.10 = f32[768,1024]{1,0:T(8,128)S(1)} fusion(f32[768,1024]{1,0:T(8,128)S(1)} %bitcast.180), kind=kOutput, calls=%fused_computation.30 | convolution fusion | flops 9678356480 | bytes 6291456 | tf_op jit(solution)/shard_map/dot_general | solution.py:37
  347.4 27.3 %fusion.14 = f32[768,1024]{1,0:T(8,128)S(1)} fusion(f32[768,1024]{1,0:T(8,128)S(1)} %bitcast.181), kind=kOutput, calls=%fused_computation.32 | convolution fusion | flops 9678356480 | bytes 6291456 | tf_op jit(solution)/shard_map/dot_general | solution.py:38
  374.7 1.0 fusion.16
  376.9 27.5 %fusion.12 = f32[768,1024]{1,0:T(8,128)S(1)} fusion(f32[768,1024]{1,0:T(8,128)S(1)} %bitcast.182), kind=kOutput, calls=%fused_computation.31 | convolution fusion | flops 9678356480 | bytes 6291456 | tf_op jit(solution)/shard_map/dot_general | solution.py:38
  404.4 27.1 %fusion.8 = f32[768,1024]{1,0:T(8,128)S(1)} fusion(f32[768,1024]{1,0:T(8,128)S(1)} %bitcast.183), kind=kOutput, calls=%fused_computation.29 | convolution fusion | flops 9678356480 | bytes 6291456 | tf_op jit(solution)/shard_map/dot_general | solution.py:37
  431.4 1.1 subtract_bitcast_fusion
  433.3 5.2 collective-permute-done.4
  438.5 1.1 add_multiply_fusion.3
  439.6 0.7 multiply_subtract_fusion.2
  440.5 6.3 collective-permute-start.5
  446.8 136.9 %collective-permute-done.5 = f32[2,384,1024]{2,1,0:T(8,128)S(1)} collective-permute-done((f32[2,384,1024]{2,1,0:T(8,128)S(1)}, f32[2,384,1024]{2,1,0:T(8,128)S(1)}, u32[]{:S(2)}, u32[]{:S(2)}) %collective-permute-start.5) | collective-permute-done | bytes 3145760 | tf_op jit(solution)/shard_map/ppermute | solution.py:18
  583.7 1.1 add_multiply_fusion.2
  584.7 0.7 multiply_subtract_fusion.1
  585.6 1.5 collective-permute-start.6
  587.2 67.4 %collective-permute-done.6 = f32[2,384,1024]{2,1,0:T(8,128)S(1)} collective-permute-done((f32[2,384,1024]{2,1,0:T(8,128)S(1)}, f32[2,384,1024]{2,1,0:T(8,128)S(1)}, u32[]{:S(2)}, u32[]{:S(2)}) %collective-permute-start.6) | collective-permute-done | bytes 3145760 | tf_op jit(solution)/shard_map/ppermute | solution.py:18
  654.6 1.1 add_multiply_fusion.1
  655.7 0.7 multiply_subtract_fusion
  656.6 2.8 collective-permute-start.7
  659.4 66.6 %collective-permute-done.7 = f32[2,384,1024]{2,1,0:T(8,128)S(1)} collective-permute-done((f32[2,384,1024]{2,1,0:T(8,128)S(1)}, f32[2,384,1024]{2,1,0:T(8,128)S(1)}, u32[]{:S(2)}, u32[]{:S(2)}) %collective-permute-start.7) | collective-permute-done | bytes 3145760 | tf_op jit(solution)/shard_map/ppermute | solution.py:18
  726.0 1.1 add_multiply_fusion
  727.3 0.7 copy-done.9
  727.9 0.7 slice_multiply_fusion
  728.9 0.9 reshape.324
  729.8 4.3 all-to-all-start.1
  734.3 0.9 reshape.322
  735.2 6.7 all-to-all-done.1
  741.8 3.5 all-to-all-start
  746.0 7.1 all-to-all-done
  753.7 0.8 fusion.51
  754.5 3.0 fusion.18
  (64 shorter events, 9.1 us)
Async XLA Ops:
  0.6 753.1 %copy-start = (bf16[1024,1024]{1,0:T(8,128)(2,1)S(1)}, bf16[1024,1024]{1,0:T(8,128)(2,1)}, u32[]{:S(2)}) copy-start(bf16[1024,1024]{1,0:T(8,128)(2,1)} %param.10) | copy-start | bytes 6291460
  3.3 2.4 copy-start.1
  3.5 2.5 copy-start.2
  5.9 70.7 %collective-permute-start = (f32[2,384,1024]{2,1,0:T(8,128)}, f32[2,384,1024]{2,1,0:T(8,128)}, u32[]{:S(2)}, u32[]{:S(2)}) collective-permute-start(f32[2,384,1024]{2,1,0:T(8,128)} %pad_maximum_fusion), channel_id=1, source_target_pairs={{0,128},{128,0},{16,144},{144,16},{32,160},{160,32},{48,176},{176,... | collective-permute-start | bytes 9437192 | tf_op jit(solution)/shard_map/ppermute | solution.py:18
  80.9 2.2 copy-start.5
  80.9 2.6 copy-start.6
  83.5 69.1 %collective-permute-start.1 = (f32[2,384,1024]{2,1,0:T(8,128)}, f32[2,384,1024]{2,1,0:T(8,128)}, u32[]{:S(2)}, u32[]{:S(2)}) collective-permute-start(f32[2,384,1024]{2,1,0:T(8,128)} %pad_maximum_fusion.1), channel_id=1, source_target_pairs={{0,64},{64,0},{16,80},{80,16},{32,96},{96,32},{48,112},{112,48},{1... | collective-permute-start | bytes 9437192 | tf_op jit(solution)/shard_map/ppermute | solution.py:18
  157.0 2.2 copy-start.3
  157.0 2.6 copy-start.4
  159.6 105.6 %collective-permute-start.2 = (f32[2,384,1024]{2,1,0:T(8,128)}, f32[2,384,1024]{2,1,0:T(8,128)}, u32[]{:S(2)}, u32[]{:S(2)}) collective-permute-start(f32[2,384,1024]{2,1,0:T(8,128)} %pad_maximum_fusion.2), channel_id=1, source_target_pairs={{0,32},{32,0},{16,48},{48,16},{64,96},{96,64},{80,112},{112,80},{1... | collective-permute-start | bytes 9437192 | tf_op jit(solution)/shard_map/ppermute | solution.py:18
  269.5 2.2 copy-start.7
  269.5 2.6 copy-start.8
  272.2 43.7 %collective-permute-start.3 = (f32[2,384,1024]{2,1,0:T(8,128)}, f32[2,384,1024]{2,1,0:T(8,128)}, u32[]{:S(2)}, u32[]{:S(2)}) collective-permute-start(f32[2,384,1024]{2,1,0:T(8,128)} %pad_maximum_fusion.3), channel_id=1, source_target_pairs={{0,16},{16,0},{32,48},{48,32},{64,80},{80,64},{96,112},{112,96},{1... | collective-permute-start | bytes 9437192 | tf_op jit(solution)/shard_map/ppermute | solution.py:18
  432.7 5.8 collective-permute-start.4
  440.5 143.2 %collective-permute-start.5 = (f32[2,384,1024]{2,1,0:T(8,128)S(1)}, f32[2,384,1024]{2,1,0:T(8,128)S(1)}, u32[]{:S(2)}, u32[]{:S(2)}) collective-permute-start(f32[2,384,1024]{2,1,0:T(8,128)S(1)} %pad_maximum_fusion.7), channel_id=1, source_target_pairs={{0,32},{32,0},{16,48},{48,16},{64,96},{96,64},{80,112},{112,80},{1... | collective-permute-start | bytes 9437192 | tf_op jit(solution)/shard_map/ppermute | solution.py:18
  585.6 69.0 %collective-permute-start.6 = (f32[2,384,1024]{2,1,0:T(8,128)S(1)}, f32[2,384,1024]{2,1,0:T(8,128)S(1)}, u32[]{:S(2)}, u32[]{:S(2)}) collective-permute-start(f32[2,384,1024]{2,1,0:T(8,128)S(1)} %pad_maximum_fusion.8), channel_id=1, source_target_pairs={{0,64},{64,0},{16,80},{80,16},{32,96},{96,32},{48,112},{112,48},{1... | collective-permute-start | bytes 9437192 | tf_op jit(solution)/shard_map/ppermute | solution.py:18
  656.6 69.4 %collective-permute-start.7 = (f32[2,384,1024]{2,1,0:T(8,128)S(1)}, f32[2,384,1024]{2,1,0:T(8,128)S(1)}, u32[]{:S(2)}, u32[]{:S(2)}) collective-permute-start(f32[2,384,1024]{2,1,0:T(8,128)S(1)} %pad_maximum_fusion.9), channel_id=1, source_target_pairs={{0,128},{128,0},{16,144},{144,16},{32,160},{160,32},{48,176},{176,... | collective-permute-start | bytes 9437192 | tf_op jit(solution)/shard_map/ppermute | solution.py:18
  727.0 0.9 copy-start.9
  729.8 12.1 %all-to-all-start.1 = ((bf16[16,2,2048]{2,1,0:T(2,128)(2,1)}), bf16[16,2,2048]{2,1,0:T(2,128)(2,1)S(1)}, u32[]{:S(2)}, u32[]{:S(2)}) async-start(bf16[16,2,2048]{2,1,0:T(2,128)(2,1)} %reshape.324), calls=%async_computation.1 | async-start | bytes 262144 | tf_op jit(solution)/shard_map/all_to_all | solution.py:149
  741.8 11.3 %all-to-all-start = ((bf16[16,2,2048]{2,1,0:T(2,128)(2,1)}), bf16[16,2,2048]{2,1,0:T(2,128)(2,1)S(1)}, u32[]{:S(2)}, u32[]{:S(2)}) async-start(bf16[16,2,2048]{2,1,0:T(2,128)(2,1)} %reshape.322), calls=%async_computation | async-start | bytes 262144 | tf_op jit(solution)/shard_map/all_to_all | solution.py:148
where the time goes:
time: 768 us; the launch traced here: 758 us
  waiting for transfers between devices  528 us (69%)
  matrix products  112 us (15%)
  starting transfers between devices  69.8 us (9%)
  other arithmetic  40.5 us (5%)
    ppermute x8, waiting for transfers between devices, from_partner(): return lax.ppermute(block, axis, route)  514 us
    ppermute x8, starting transfers between devices, from_partner(): return lax.ppermute(block, axis, route)  62 us
    dot_general x2, matrix products, local_dft(): jnp.dot(flat, sin_tab, precision=exact_mode).reshape(2, rows, seq_len)  54.7 us
    dot_general x2, matrix products, local_dft(): jnp.dot(flat, cos_tab, precision=exact_mode).reshape(2, rows, seq_len)  53.9 us
    add x4, other arithmetic, forward_pairs(): mixed = other + sign * stacked  15.4 us
  transfers between devices with their start and end apart: 10, of which 10 were waited for; matrix products, arithmetic and copies ran while one was open for 0% of the time, Pallas kernels for 0%

commit v1 on v0

v1 whole, which is shorter than its diff:
```python
import numpy as np

import jax
import jax.numpy as jnp
import ml_dtypes
from jax import lax
from jax.sharding import PartitionSpec as P


def dft_matrix(block):
    order = np.concatenate([np.arange(0, block, 2), np.arange(1, block, 2)])
    steps = (2 * order + 1)[None, :] * np.arange(block)[:, None] % (4 * block)
    angle = np.pi * steps / (2 * block)
    return np.concatenate([np.cos(angle), -np.sin(angle)], 1).astype(ml_dtypes.bfloat16)


def local(values, gate_acts, cotangent, filter_taps, w_value, w_gate):
    n_seq = lax.axis_size("seq")
    channels, block = values.shape
    mine = channels // n_seq
    total = block * n_seq
    bf16 = jnp.bfloat16
    f32 = jnp.float32
    table = jnp.asarray(dft_matrix(block))
    upstream = (cotangent.astype(f32) * gate_acts.astype(f32)).astype(bf16)
    packed = jnp.stack([values, upstream, filter_taps.astype(bf16), cotangent])
    packed = packed.reshape(4, n_seq, mine, block).transpose(1, 0, 2, 3)
    got = lax.all_to_all(packed, "seq", split_axis=0, concat_axis=0, tiled=True)
    spectra = lax.dot_general(
        got[:, :3], table, (((3,), (0,)), ((), ())), preferred_element_type=f32
    )
    re = spectra[..., :block]
    im = spectra[..., block:]
    half = block // 2
    sign = jnp.where(jnp.arange(block) < half, 1.0, -1.0)

    def conv(p, q):
        (pr, pi), (qr, qi) = p, q
        out_r = 0.0
        out_i = 0.0
        for c in range(n_seq):
            pad = ((c, 0), (0, 0), (0, 0))
            sr = jnp.pad(qr[: n_seq - c], pad)
            si = jnp.pad(qi[: n_seq - c], pad)
            out_r = out_r + (pr[c] * sr - pi[c] * si)
            out_i = out_i + (pr[c] * si + pi[c] * sr)
        pad = ((1, 0), (0, 0), (0, 0))
        before_r = jnp.pad(out_r[:-1], pad)
        before_i = jnp.pad(out_i[:-1], pad)
        return out_r - sign * before_i, out_i + sign * before_r

    def corr(p, q):
        (pr, pi), (qr, qi) = p, q
        out_r = 0.0
        out_i = 0.0
        for c in range(n_seq):
            pad = ((0, c), (0, 0), (0, 0))
            sr = jnp.pad(qr[c:], pad)
            si = jnp.pad(qi[c:], pad)
            out_r = out_r + (pr[c] * sr + pi[c] * si)
            out_i = out_i + (pr[c] * si - pi[c] * sr)
        pad = ((0, 1), (0, 0), (0, 0))
        after_r = jnp.pad(out_r[1:], pad)
        after_i = jnp.pad(out_i[1:], pad)
        return out_r + sign * after_i, out_i - sign * after_r

    v = (re[:, 0], im[:, 0])
    u = (re[:, 1], im[:, 1])
    h = (re[:, 2], im[:, 2])
    triples = [conv(h, v), corr(h, u), corr(v, u)]
    products = jnp.stack([jnp.concatenate(t, -1).astype(bf16) for t in triples], 1)
    signals = lax.dot_general(
        products, table, (((3,), (1,)), ((), ())), preferred_element_type=f32
    )
    signals = signals * (1.0 / (block * total**0.5))
    gate_grad = got[:, 3].astype(f32) * signals[:, 0]
    back = jnp.stack([signals[:, 1], gate_grad, signals[:, 2]], 1).astype(bf16)
    back = lax.all_to_all(back, "seq", split_axis=0, concat_axis=0, tiled=True)
    back = back.transpose(1, 0, 2, 3).reshape(3, channels, block)
    grads = lax.all_to_all(back[:2], "chan", split_axis=2, concat_axis=1, tiled=True)
    contract = (((0,), (1,)), ((), ()))
    input_grad = lax.dot_general(grads[0], w_value, contract, preferred_element_type=f32)
    input_grad = input_grad + lax.dot_general(
        grads[1], w_gate, contract, preferred_element_type=f32
    )
    return (input_grad.astype(bf16), back[2].astype(f32))


def solution(mesh):
    return jax.shard_map(
        local,
        mesh=mesh,
        in_specs=(P("chan", "seq"), P("chan", "seq"), P("chan", "seq"), P("chan", "seq"), P(), P()),
        out_specs=(P(("seq", "chan"), None), P("chan", "seq")),
        check_vma=False,
    )
```

time: 768 us -> 94.9 us (0.12); the launches traced: 758 us -> 94.4 us
  waiting for transfers between devices: 528 us -> 23.8 us
  matrix products: 112 us -> 7.09 us
  starting transfers between devices: 69.8 us -> 23.5 us
  other arithmetic: 40.5 us -> 10.9 us
  blocking collectives: 0 us -> 15.9 us
    ppermute x8 -> x0, waiting for transfers between devices: 514 us -> none  [from_partner(): return lax.ppermute(block, axis, route)]
    dot_general x6 -> x4, matrix products: 112 us -> 7.09 us  [the longest x1 3.2 us: local(): lax.dot_general(got[:, :3], table, (((3,), (0,)), ((), ())), preferred_el...]
    ppermute x8 -> x0, starting transfers between devices: 62 us -> none  [from_partner(): return lax.ppermute(block, axis, route)]
    all_to_all x0 -> x1, blocking collectives: none -> 15.9 us  [local(): back = lax.all_to_all(back, 'seq', split_axis=0, concat_axis=0, tiled=True)]
    all_to_all x2, starting transfers between devices: 7.81 us -> 23.5 us  [the longest x1 12.4 us: local(): got = lax.all_to_all(packed, 'seq', split_axis=0, concat_axis=0, tiled=True)]
    add x4 -> x3, other arithmetic: 15.4 us -> 4.03 us  [the longest x2 2.29 us: corr(): out_i = out_i + (pr[c] * si - pi[c] * sr)]
    another operation x11 -> x2, other arithmetic: 10.5 us -> 0.11 us  [the longest x4 6.84 us: forward_pairs(): stacked = jnp.stack([real_part, imag_part])]
    all_to_all x2, waiting for transfers between devices: 13.8 us -> 23.8 us  [the longest x1 14.9 us: local(): got = lax.all_to_all(packed, 'seq', split_axis=0, concat_axis=0, tiled=True)]
  transfers between devices with their start and end apart: 10 -> 2, of which waited for: 10 -> 2; matrix products, arithmetic and copies ran while one was open for 0% -> 1% of each run, Pallas kernels for 0% -> 0%
where the time goes in v1:
time: 94.9 us; the launch traced here: 94.4 us
  waiting for transfers between devices  23.8 us (25%)
  starting transfers between devices  23.5 us (25%)
  blocking collectives  15.9 us (17%)
  local copies, waits for them, and re-layouts  11.9 us (13%)
  other arithmetic  10.9 us (11%)
  matrix products  7.09 us (7%)
  between operations  1.26 us (1%)
    all_to_all x1, blocking collectives, local(): back = lax.all_to_all(back, 'seq', split_axis=0, concat_axis=0, tiled=True)  15.9 us
    all_to_all x1, waiting for transfers between devices, local(): got = lax.all_to_all(packed, 'seq', split_axis=0, concat_axis=0, tiled=True)  14.9 us
    all_to_all x1, starting transfers between devices, local(): got = lax.all_to_all(packed, 'seq', split_axis=0, concat_axis=0, tiled=True)  12.4 us
    all_to_all x1, starting transfers between devices, local(): lax.all_to_all(back[:2], 'chan', split_axis=2, concat_axis=1, tiled=True)  11.1 us
    all_to_all x1, waiting for transfers between devices, local(): lax.all_to_all(back[:2], 'chan', split_axis=2, concat_axis=1, tiled=True)  8.92 us
    concatenate x4, other arithmetic, local(): jnp.concatenate(t, -1).astype(bf16)  4.34 us
    unnamed x40, local copies, waits for them, and re-layouts  3.42 us
    dot_general x1, matrix products, local(): lax.dot_general(got[:, :3], table, (((3,), (0,)), ((), ())), preferred_el...  3.2 us
  transfers between devices with their start and end apart: 2, of which 2 were waited for; matrix products, arithmetic and copies ran while one was open for 1% of the time, Pallas kernels for 0%

profile of v1, /device:TPU:1, one launch (start us, length us, event | category | flops | bytes accessed | tf_op | source)
XLA Modules:
  0.0 94.4 jit_solution(6180328612691542865)
XLA Ops:
  0.6 1.1 %stack.26 = bf16[1,16,4,1024]{3,2,1,0:T(4,128)(2,1)S(1)} reshape(bf16[64,1024]{1,0:T(8,128)(2,1)} %param.7) | data formatting | bytes 262144 | tf_op jit(solution)/shard_map/stack | solution.py:26
  1.8 1.0 %stack.29 = bf16[1,16,4,1024]{3,2,1,0:T(4,128)(2,1)S(1)} reshape(bf16[64,1024]{1,0:T(8,128)(2,1)} %param.9) | data formatting | bytes 262144 | tf_op jit(solution)/shard_map/stack | solution.py:26
  2.7 1.0 %multiply_convert_fusion = bf16[64,1024]{1,0:T(8,128)(2,1)S(1)} fusion(bf16[64,1024]{1,0:T(8,128)(2,1)} %param.8, bf16[64,1024]{1,0:T(8,128)(2,1)} %param.9), kind=kLoop, calls=%fused_computation.250 | loop fusion | flops 262144 | bytes 393216 | tf_op jit(solution)/shard_map/convert_element_type | solution.py:25
  3.7 0.1 stack.27
  3.8 1.0 %convert_element_type.179 = bf16[64,1024]{1,0:T(8,128)(2,1)S(1)} convert(f32[64,1024]{1,0:T(8,128)} %param.10) | non-fusion elementwise | flops 65536 | bytes 393216 | tf_op jit(solution)/shard_map/convert_element_type | solution.py:26
  4.8 0.1 stack.28
  4.8 0.5 maximum_bitcast_fusion
  5.3 1.1 %copy.23 = bf16[16,4,4,1024]{3,2,1,0:T(4,128)(2,1)} copy(bf16[16,4,4,1024]{3,2,0,1:T(4,128)(2,1)S(1)} %maximum_bitcast_fusion) | data formatting | bytes 1048576 | tf_op jit(solution)/shard_map/transpose | solution.py:27
  6.4 12.4 %all-to-all-start = ((bf16[16,4,4,1024]{3,2,1,0:T(4,128)(2,1)}), bf16[16,4,4,1024]{3,2,1,0:T(4,128)(2,1)S(1)}, u32[]{:S(2)}, u32[]{:S(2)}) async-start(bf16[16,4,4,1024]{3,2,1,0:T(4,128)(2,1)} %copy.23), calls=%async_computation | async-start | bytes 1048576 | tf_op jit(solution)/shard_map/all_to_all | solution.py:28
  18.8 14.9 %all-to-all-done = bf16[16,4,4,1024]{3,2,1,0:T(4,128)(2,1)S(1)} async-done(((bf16[16,4,4,1024]{3,2,1,0:T(4,128)(2,1)}), bf16[16,4,4,1024]{3,2,1,0:T(4,128)(2,1)S(1)}, u32[]{:S(2)}, u32[]{:S(2)}) %all-to-all-start) | async-done | bytes 524320 | tf_op jit(solution)/shard_map/all_to_all | solution.py:28
  33.7 0.1 slice.1167
  33.8 3.2 %fusion.10 = f32[16,3,4,2048]{3,0,2,1:T(8,128)S(1)} fusion(bf16[1024,2048,1,1]{1,0,3,2:T(8,128)(2,1)} %constant.146, bf16[16,3,4,1024]{3,2,1,0:T(4,128)(2,1)S(1)} %slice.1167), kind=kOutput, calls=%fused_computation.80 | convolution fusion | flops 805306368 | bytes 6160384 | tf_op jit(solution)/shard_map/dot_general | solution.py:29
  37.1 0.1 fusion.123
  37.4 0.3 fusion.122
  37.7 0.3 fusion.121
  38.0 0.3 fusion.120
  38.5 0.1 slice_bitcast_fusion.21
  38.6 0.1 slice_bitcast_fusion.23
  38.7 0.1 slice_bitcast_fusion.17
  38.9 0.1 slice_bitcast_fusion.25
  39.0 0.1 slice_bitcast_fusion.27
  39.1 0.1 slice_bitcast_fusion.19
  39.3 0.1 slice_bitcast_fusion.29
  39.7 1.1 %fusion.79 = f32[16,4,1024]{2,0,1:T(8,128)S(1)} fusion(f32[8,4,1024]{2,0,1:T(8,128)S(1)} %get-tuple-element.64, f32[8,4,1024]{2,0,1:T(8,128)S(1)} %get-tuple-element.63, f32[7,4,1024]{2,0,1:T(8,128)S(1)} %get-tuple-element.60, f32[7,4,1024]{2,0,1:T(8,128)S(1)} %get-tuple-element.59, f32[6,4,1024]{2,0,1:T(8,128)S(1)} %get-tuple-element.56, ...), kind=kLoop, calls=%fused_computation.181 | loop fusion | flops 4128768 | bytes 5242880 | tf_op jit(solution)/shard_map/add | solution.py:61
  41.2 1.1 %fusion.61 = f32[16,4,1024]{2,0,1:T(8,128)S(1)} fusion(f32[8,4,1024]{2,0,1:T(8,128)S(1)} %get-tuple-element.64, f32[8,4,1024]{2,0,1:T(8,128)S(1)} %get-tuple-element.63, f32[7,4,1024]{2,0,1:T(8,128)S(1)} %get-tuple-element.60, f32[7,4,1024]{2,0,1:T(8,128)S(1)} %get-tuple-element.59, f32[6,4,1024]{2,0,1:T(8,128)S(1)} %get-tuple-element.56, ...), kind=kLoop, calls=%fused_computation.163 | loop fusion | flops 4128768 | bytes 5242880 | tf_op jit(solution)/shard_map/add | solution.py:61
  42.3 1.7 %fusion.29 = f32[16,4,1024]{2,0,1:T(8,128)S(1)} fusion(f32[8,4,1024]{2,0,1:T(8,128)S(1)} %get-tuple-element.65, f32[8,4,1024]{2,0,1:T(8,128)S(1)} %get-tuple-element.62, f32[7,4,1024]{2,0,1:T(8,128)S(1)} %get-tuple-element.61, f32[7,4,1024]{2,0,1:T(8,128)S(1)} %get-tuple-element.58, f32[6,4,1024]{2,0,1:T(8,128)S(1)} %get-tuple-element.57, ...), kind=kLoop, calls=%fused_computation.131 | loop fusion | flops 4128768 | bytes 5242880 | tf_op jit(solution)/shard_map/add | solution.py:46
  44.1 1.8 %fusion.109 = (bf16[16,1,4,1024]{3,0,2,1:T(8,128)(2,1)S(1)}, f32[16,4,1024]{2,0,1:T(8,128)S(1)}) fusion(f32[15,4,1024]{2,0,1:T(8,128)S(1)} %bitcast.329, f32[1024]{0:T(1024)S(1)} %fusion.115, f32[1,4,1024]{2,0,1:T(1,128)S(1)} %get-tuple-element.36, f32[4,1024]{1,0:T(4,128)S(1)} %get-tuple-element.155, f32[1,4,1024]{2,0,1:T(1,128)S(1)} %get-tuple-element.37, ...), kind=kLoop, calls=%fused_computation.251 | loop fusion | flops 4325376 | bytes 5623808 | tf_op jit(solution)/shard_map/concatenate | solution.py:71
  45.8 1.2 %fusion.113 = (bf16[16,1,4,1024]{3,0,2,1:T(8,128)(2,1)S(1)}, f32[16,4,1024]{2,0,1:T(8,128)S(1)}) fusion(f32[15,4,1024]{2,0,1:T(8,128)S(1)} %slice.1298, f32[1024]{0:T(1024)S(1)} %fusion.115, f32[1,4,1024]{2,0,1:T(1,128)S(1)} %get-tuple-element.98, f32[4,1024]{1,0:T(4,128)S(1)} %get-tuple-element.183, f32[1,4,1024]{2,0,1:T(1,128)S(1)} %get-tuple-element.99, ...), kind=kLoop, calls=%fused_computation.255 | loop fusion | flops 4325376 | bytes 5623808 | tf_op jit(solution)/shard_map/concatenate | solution.py:71
  47.1 1.2 %fusion.111 = (bf16[16,1,4,1024]{3,0,2,1:T(8,128)(2,1)S(1)}, f32[16,4,1024]{2,0,1:T(8,128)S(1)}) fusion(f32[15,4,1024]{2,0,1:T(8,128)S(1)} %slice.1266, f32[1024]{0:T(1024)S(1)} %fusion.115, f32[1,4,1024]{2,0,1:T(1,128)S(1)} %get-tuple-element.98, f32[4,1024]{1,0:T(4,128)S(1)} %get-tuple-element.155, f32[1,4,1024]{2,0,1:T(1,128)S(1)} %get-tuple-element.99, ...), kind=kLoop, calls=%fused_computation.253 | loop fusion | flops 4325376 | bytes 5623808 | tf_op jit(solution)/shard_map/concatenate | solution.py:71
  48.4 0.2 fusion.110
  48.5 0.8 copy-done.1
  49.3 1.7 %fusion.126 = (bf16[16,3,4,1024]{3,0,2,1:T(8,128)(2,1)S(1)}, f32[16,3,4,1024]{3,0,2,1:T(8,128)S(1)}) fusion(bf16[1024,2048,1,1]{1,0,3,2:T(8,128)(2,1)S(1)} %copy-done.1, bf16[16,1,4,1024]{3,0,2,1:T(8,128)(2,1)S(1)} %get-tuple-element.138, bf16[16,1,4,1024]{3,0,2,1:T(8,128)(2,1)S(1)} %get-tuple-element.6, ...), kind=kOutput, calls=%fused_computation.363 | convolution fusion | flops 810418176 | bytes 6160384 | tf_op jit(solution)/shard_map/dot_general | solution.py:72
  51.2 0.3 copy.26
  51.5 15.9 %all_to_all.25 = bf16[16,3,4,1024]{3,2,1,0:T(4,128)(2,1)S(1)} all-to-all(bf16[16,3,4,1024]{3,2,1,0:T(4,128)(2,1)S(1)} %copy.26), channel_id=1, replica_groups=mesh['seq'=16,'chan'=16] {'seq'}, dimensions={0} | all-to-all | bytes 786432 | tf_op jit(solution)/shard_map/all_to_all | solution.py:78
  67.4 0.1 slice.1304
  67.5 0.2 copy.27
  67.8 0.5 copy.28
  68.2 1.1 %reshape.309 = bf16[16,2,4096]{2,1,0:T(2,128)(2,1)} reshape(bf16[1024,2,64]{2,1,0:T(2,128)(2,1)S(1)} %bitcast.330) | data formatting | bytes 524288
  69.4 11.1 %all-to-all-start.2 = ((bf16[16,2,4096]{2,1,0:T(2,128)(2,1)}), bf16[16,2,4096]{2,1,0:T(2,128)(2,1)S(1)}, u32[]{:S(2)}, u32[]{:S(2)}) async-start(bf16[16,2,4096]{2,1,0:T(2,128)(2,1)} %reshape.309), calls=%async_computation.2 | async-start | bytes 524288 | tf_op jit(solution)/shard_map/all_to_all | solution.py:80
  80.5 0.8 reshape.307
  81.3 8.9 %all-to-all-done.2 = bf16[16,2,4096]{2,1,0:T(2,128)(2,1)S(1)} async-done(((bf16[16,2,4096]{2,1,0:T(2,128)(2,1)}), bf16[16,2,4096]{2,1,0:T(2,128)(2,1)S(1)}, u32[]{:S(2)}, u32[]{:S(2)}) %all-to-all-start.2) | async-done | bytes 262176 | tf_op jit(solution)/shard_map/all_to_all | solution.py:80
  90.2 0.3 reshape.310
  90.6 0.3 copy.165
  91.0 0.2 squeeze.28
  91.2 0.2 squeeze.27
  91.4 0.8 fusion.127
  92.1 0.8 copy-done.2
  93.0 1.4 %fusion = bf16[64,1024]{1,0:T(8,128)(2,1)} fusion(f32[64,1024]{1,0:T(8,128)S(1)} %fusion.127, bf16[1024,64]{0,1:T(8,128)(2,1)S(1)} %squeeze.28, bf16[1024,1024]{1,0:T(8,128)(2,1)S(1)} %copy-done.2), kind=kOutput, calls=%fused_computation.2 | convolution fusion | flops 134348800 | bytes 2621440 | tf_op jit(solution)/shard_map/dot_general | solution.py:83
  (55 shorter events, 1.0 us)
Async XLA Ops:
  0.6 90.7 %copy-start = (bf16[1024,1024]{1,0:T(8,128)(2,1)S(1)}, bf16[1024,1024]{1,0:T(8,128)(2,1)}, u32[]{:S(2)}) copy-start(bf16[1024,1024]{1,0:T(8,128)(2,1)} %param.11) | copy-start | bytes 6291460
  6.4 27.3 %all-to-all-start = ((bf16[16,4,4,1024]{3,2,1,0:T(4,128)(2,1)}), bf16[16,4,4,1024]{3,2,1,0:T(4,128)(2,1)S(1)}, u32[]{:S(2)}, u32[]{:S(2)}) async-start(bf16[16,4,4,1024]{3,2,1,0:T(4,128)(2,1)} %copy.23), calls=%async_computation | async-start | bytes 1048576 | tf_op jit(solution)/shard_map/all_to_all | solution.py:28
  47.1 2.2 %copy-start.1 = (bf16[1024,2048,1,1]{1,0,3,2:T(8,128)(2,1)S(1)}, bf16[1024,2048,1,1]{1,0,3,2:T(8,128)(2,1)}, u32[]{:S(2)}) copy-start(bf16[1024,2048,1,1]{1,0,3,2:T(8,128)(2,1)} %constant.146) | copy-start | bytes 12582916
  69.4 20.9 %all-to-all-start.2 = ((bf16[16,2,4096]{2,1,0:T(2,128)(2,1)}), bf16[16,2,4096]{2,1,0:T(2,128)(2,1)S(1)}, u32[]{:S(2)}, u32[]{:S(2)}) async-start(bf16[16,2,4096]{2,1,0:T(2,128)(2,1)} %reshape.309), calls=%async_computation.2 | async-start | bytes 524288 | tf_op jit(solution)/shard_map/all_to_all | solution.py:80
  91.4 1.6 %copy-start.2 = (bf16[1024,1024]{1,0:T(8,128)(2,1)S(1)}, bf16[1024,1024]{1,0:T(8,128)(2,1)}, u32[]{:S(2)}) copy-start(bf16[1024,1024]{1,0:T(8,128)(2,1)} %param.12) | copy-start | bytes 6291460

commit v2 on v1

v2 whole, which is shorter than its diff:
```python
import functools

import numpy as np

import jax
import jax.numpy as jnp
import ml_dtypes
from jax import lax
from jax.experimental import pallas as pl
from jax.experimental.pallas import tpu as pltpu
from jax.sharding import PartitionSpec as P

MESH = pl.DeviceIdType.MESH
LANES = 128
MINE = 4


def dft_tables(block):
    chunks = block // LANES
    order = np.concatenate([np.arange(0, block, 2), np.arange(1, block, 2)])
    steps = (2 * order + 1)[None, :] * np.arange(block)[:, None] % (4 * block)
    angle = np.pi * steps / (2 * block)
    table = np.stack([np.cos(angle), -np.sin(angle)]).reshape(2, block, chunks, LANES)
    table = table.transpose(2, 1, 0, 3).reshape(chunks, block, 2 * LANES)
    high = table.astype(ml_dtypes.bfloat16)
    low = (table - high.astype(np.float64)).astype(ml_dtypes.bfloat16)
    return high, low


def kernel(
    n_seq,
    n_chan,
    values,
    gates,
    cotangent,
    taps,
    high_hbm,
    low_hbm,
    wv_hbm,
    wg_hbm,
    input_grad,
    filter_grad,
    high,
    low,
    wv,
    wg,
    flat,
    send_hv,
    send_uc,
    got_hv,
    got_uc,
    rows,
    spec,
    swapped,
    prod,
    packed,
    signal,
    send_g,
    send_f,
    got_g,
    got_f,
    tiles,
    stacked,
    load_sem,
    own_sem,
    hv_send,
    hv_recv,
    uc_send,
    uc_recv,
    g_send,
    g_recv,
    f_send,
    f_recv,
    t_send,
    t_recv,
):
    f32 = jnp.float32
    bf16 = jnp.bfloat16
    me = lax.axis_index("seq")
    my_chan = lax.axis_index("chan")
    block = values.shape[1]
    chunks = block // LANES
    share = block // n_chan

    barrier = pltpu.get_barrier_semaphore()

    def greet_seq(k, carry):
        pl.semaphore_signal(
            barrier, inc=1, device_id={"seq": me ^ k}, device_id_type=MESH
        )
        return carry

    def greet_chan(k, carry):
        pl.semaphore_signal(
            barrier, inc=1, device_id={"chan": my_chan ^ k}, device_id_type=MESH
        )
        return carry

    lax.fori_loop(1, n_seq, greet_seq, 0)
    lax.fori_loop(1, n_chan, greet_chan, 0)

    loads = [
        pltpu.make_async_copy(src, dst, load_sem.at[i])
        for i, (src, dst) in enumerate(
            ((high_hbm, high), (low_hbm, low), (wv_hbm, wv), (wg_hbm, wg))
        )
    ]
    for load in loads:
        load.start()

    flat[0] = taps[...]
    flat[1] = values[...].astype(f32)
    cot = cotangent[...].astype(f32)
    flat[2] = cot * gates[...].astype(f32)
    flat[3] = cot

    def pack(t, carry):
        at = pl.ds(pl.multiple_of(t * 8, 8), 8)
        h, v, u, c = (flat[i, at, :] for i in range(4))
        for side in range(2):
            part = slice(side * MINE, side * MINE + MINE)
            hv = jnp.concatenate([h[part], v[part]], 0)
            uc = jnp.concatenate([u[part], c[part]], 0)
            send_hv[2 * t + side] = hv.astype(bf16)
            send_uc[2 * t + side] = uc.astype(bf16)
        return carry

    lax.fori_loop(0, n_seq // 2, pack, 0)
    pl.semaphore_wait(barrier, n_seq + n_chan - 2)

    def to_seq(src, dst, send_sem, recv_sem, peer, slot):
        return pltpu.make_async_remote_copy(
            src_ref=src.at[peer],
            dst_ref=dst.at[slot],
            send_sem=send_sem.at[peer],
            recv_sem=recv_sem.at[slot],
            device_id={"seq": peer},
            device_id_type=MESH,
        )

    def send_all(src, dst, send_sem, recv_sem):
        def step(k, carry):
            to_seq(src, dst, send_sem, recv_sem, me ^ k, me).start()
            return carry

        lax.fori_loop(1, n_seq, step, 0)

    def wait_all(src, dst, send_sem, recv_sem):
        def step(k, carry):
            copy = to_seq(src, dst, send_sem, recv_sem, me ^ k, me ^ k)
            copy.wait_send()
            copy.wait_recv()
            return carry

        lax.fori_loop(1, n_seq, step, 0)

    own_hv = pltpu.make_async_copy(send_hv.at[me], got_hv.at[me], own_sem.at[0])
    own_uc = pltpu.make_async_copy(send_uc.at[me], got_uc.at[me], own_sem.at[1])
    send_all(send_hv, got_hv, hv_send, hv_recv)
    send_all(send_uc, got_uc, uc_send, uc_recv)
    own_hv.start()
    own_uc.start()
    loads[0].wait()
    loads[1].wait()
    own_hv.wait()
    own_uc.wait()
    wait_all(send_hv, got_hv, hv_send, hv_recv)
    wait_all(send_uc, got_uc, uc_send, uc_recv)

    def build(a, carry):
        u = got_uc[a].astype(f32)[:MINE]
        tile = jnp.concatenate([got_hv[a].astype(f32), u, u], 0)
        rows[pl.ds(pl.multiple_of(a * 16, 16), 16), :] = tile.astype(bf16)
        return carry

    lax.fori_loop(0, n_seq, build, 0)

    re = slice(0, LANES)
    im = slice(LANES, 2 * LANES)
    group = 4

    def frequency(j, carry):
        lhs = rows[...]
        spec[...] = jnp.dot(lhs, high[j], preferred_element_type=f32) + jnp.dot(
            lhs, low[j], preferred_element_type=f32
        )
        sign = jnp.where(j < chunks // 2, 1.0, -1.0).astype(f32)

        def first(a):
            at = slice(a * 16, a * 16 + 8)
            return spec[at, re], spec[at, im]

        def second(a):
            at = slice(a * 16 + 8, a * 16 + 16)
            return spec[at, re], spec[at, im]

        for a in range(n_seq):
            at = slice(a * 8, a * 8 + 8)
            pr, pi = first(a)
            swapped[at, re] = pltpu.roll(pr, 4, axis=0)
            swapped[at, im] = pltpu.roll(pi, 4, axis=0)

        def turned(a):
            at = slice(a * 8, a * 8 + 8)
            return swapped[at, re], swapped[at, im]

        before = None
        for base in range(0, n_seq, group):
            acc = [None] * group
            for x in range((base + group - 1) // 2 + 1):
                pr, pi = first(x)
                for i in range(group):
                    y = base + i - x
                    if y < x:
                        continue
                    qr, qi = turned(y)
                    if y == x:
                        ar, ai = pr * 0.5, pi * 0.5
                    else:
                        ar, ai = pr, pi
                    tr = ar * qr - ai * qi
                    ti = ar * qi + ai * qr
                    acc[i] = (tr, ti) if acc[i] is None else (acc[i][0] + tr, acc[i][1] + ti)
            for i in range(group):
                zr, zi = acc[i]
                at = slice((base + i) * 16, (base + i) * 16 + 8)
                if before is None:
                    prod[at, re] = zr
                    prod[at, im] = zi
                else:
                    prod[at, re] = zr - sign * before[1]
                    prod[at, im] = zi + sign * before[0]
                before = (zr, zi)

        after = None
        for base in reversed(range(0, n_seq, group)):
            acc = [None] * group
            for c in range(n_seq - base):
                pr, pi = first(c)
                for i in range(group):
                    if base + i + c >= n_seq:
                        continue
                    qr, qi = second(base + i + c)
                    tr = pr * qr + pi * qi
                    ti = pr * qi - pi * qr
                    acc[i] = (tr, ti) if acc[i] is None else (acc[i][0] + tr, acc[i][1] + ti)
            for i in reversed(range(group)):
                zr, zi = acc[i]
                at = slice((base + i) * 16 + 8, (base + i) * 16 + 16)
                if after is None:
                    prod[at, re] = zr
                    prod[at, im] = zi
                else:
                    prod[at, re] = zr + sign * after[1]
                    prod[at, im] = zi - sign * after[0]
                after = (zr, zi)
        packed[j] = prod[...].astype(bf16)
        return carry

    lax.fori_loop(0, chunks, frequency, 0)

    wide = 256
    turn = (((1,), (1,)), ((), ()))

    def inverse(t, carry):
        at = pl.ds(pl.multiple_of(t * wide, wide), wide)
        total = None
        for j in range(chunks):
            lhs = packed[j]
            part = lax.dot_general(lhs, high[j, at, :], turn, preferred_element_type=f32)
            part = part + lax.dot_general(
                lhs, low[j, at, :], turn, preferred_element_type=f32
            )
            total = part if total is None else total + part
        signal[:, at] = total * (1.0 / (block * 128.0))
        return carry

    lax.fori_loop(0, block // wide, inverse, 0)

    low_lanes = lax.broadcasted_iota(jnp.int32, (MINE, LANES), 1) < share

    def finish(a):
        both = signal[pl.ds(pl.multiple_of(a * 16, 8), 8), :]
        grads = signal[pl.ds(pl.multiple_of(a * 16 + 8, 8), 8), :]
        conv = both[:MINE] + both[MINE:]
        cots = got_uc[a].astype(f32)[MINE:]
        gate_grad = conv * cots
        value_grad = grads[:MINE]
        send_f[a] = grads[MINE:].astype(bf16)
        for p in range(block // LANES):
            at = slice(p * LANES, (p + 1) * LANES)
            x = value_grad[:, at]
            y = gate_grad[:, at]
            even = jnp.where(low_lanes, x, pltpu.roll(y, share, axis=1))
            odd = jnp.where(low_lanes, pltpu.roll(x, share, axis=1), y)
            send_g[a, :, 2 * p * LANES : (2 * p + 1) * LANES] = even.astype(bf16)
            send_g[a, :, (2 * p + 1) * LANES : (2 * p + 2) * LANES] = odd.astype(bf16)

    own_g = pltpu.make_async_copy(send_g.at[me], got_g.at[me], own_sem.at[2])
    own_f = pltpu.make_async_copy(send_f.at[me], got_f.at[me], own_sem.at[3])

    def finish_and_send(k, carry):
        finish(me ^ k)
        to_seq(send_g, got_g, g_send, g_recv, me ^ k, me).start()
        return carry

    lax.fori_loop(1, n_seq, finish_and_send, 0)
    finish(me)
    own_g.start()
    own_f.start()
    send_all(send_f, got_f, f_send, f_recv)
    own_g.wait()
    wait_all(send_g, got_g, g_send, g_recv)

    def to_chan(peer, slot):
        at = pl.ds(pl.multiple_of(peer * LANES, LANES), LANES)
        return pltpu.make_async_remote_copy(
            src_ref=got_g.at[:, :, at],
            dst_ref=tiles.at[slot],
            send_sem=t_send.at[peer],
            recv_sem=t_recv.at[slot],
            device_id={"chan": peer},
            device_id_type=MESH,
        )

    def send_tiles(k, carry):
        to_chan(my_chan ^ k, my_chan).start()
        return carry

    lax.fori_loop(1, n_chan, send_tiles, 0)
    mine_at = pl.ds(pl.multiple_of(my_chan * LANES, LANES), LANES)
    own_t = pltpu.make_async_copy(got_g.at[:, :, mine_at], tiles.at[my_chan], own_sem.at[4])
    own_t.start()

    own_f.wait()
    wait_all(send_f, got_f, f_send, f_recv)

    def unpack(t, carry):
        at = pl.ds(pl.multiple_of(t * 8, 8), 8)
        pair = [got_f[2 * t + side].astype(f32) for side in range(2)]
        filter_grad[at, :] = jnp.concatenate(pair, 0)
        return carry

    lax.fori_loop(0, n_seq // 2, unpack, 0)
    loads[2].wait()
    loads[3].wait()
    own_t.wait()

    def wait_tiles(k, carry):
        copy = to_chan(my_chan ^ k, my_chan ^ k)
        copy.wait_send()
        copy.wait_recv()
        return carry

    lax.fori_loop(1, n_chan, wait_tiles, 0)

    def restack(c, carry):
        for q in range(n_seq // 4):
            tile = jnp.concatenate(
                [tiles[c, 4 * q + i].astype(f32) for i in range(4)], 0
            )
            at = pl.ds(pl.multiple_of(c * 64 + q * 16, 16), 16)
            stacked[at, :] = tile.astype(bf16)
        return carry

    lax.fori_loop(0, n_chan, restack, 0)
    tokens = stacked[...].T
    out = lax.dot_general(tokens[:share], wv[...], turn, preferred_element_type=f32)
    out = out + lax.dot_general(tokens[share:], wg[...], turn, preferred_element_type=f32)
    input_grad[...] = out.astype(bf16)


def solution(mesh):
    n_seq = mesh.shape["seq"]
    n_chan = mesh.shape["chan"]
    bf16 = jnp.bfloat16
    f32 = jnp.float32

    def local(values, gate_acts, cotangent, filter_taps, w_value, w_gate):
        channels, block = values.shape
        chunks = block // LANES
        model = w_value.shape[0]
        high, low = dft_tables(block)
        vmem = pl.BlockSpec(memory_space=pltpu.VMEM)
        anywhere = pl.BlockSpec(memory_space=pl.ANY)
        sems = pltpu.SemaphoreType.DMA
        return pl.pallas_call(
            functools.partial(kernel, n_seq, n_chan),
            out_shape=(
                jax.ShapeDtypeStruct((block // n_chan, model), bf16),
                jax.ShapeDtypeStruct((channels, block), f32),
            ),
            in_specs=[vmem] * 4 + [anywhere] * 4,
            out_specs=(vmem, vmem),
            scratch_shapes=[
                pltpu.VMEM((chunks, block, 2 * LANES), bf16),
                pltpu.VMEM((chunks, block, 2 * LANES), bf16),
                pltpu.VMEM((model, model), bf16),
                pltpu.VMEM((model, model), bf16),
                pltpu.VMEM((4, channels, block), f32),
                pltpu.VMEM((n_seq, 8, block), bf16),
                pltpu.VMEM((n_seq, 8, block), bf16),
                pltpu.VMEM((n_seq, 8, block), bf16),
                pltpu.VMEM((n_seq, 8, block), bf16),
                pltpu.VMEM((n_seq * 16, block), bf16),
                pltpu.VMEM((n_seq * 16, 2 * LANES), f32),
                pltpu.VMEM((n_seq * 8, 2 * LANES), f32),
                pltpu.VMEM((n_seq * 16, 2 * LANES), f32),
                pltpu.VMEM((chunks, n_seq * 16, 2 * LANES), bf16),
                pltpu.VMEM((n_seq * 16, block), f32),
                pltpu.VMEM((n_seq, MINE, 2 * block), bf16),
                pltpu.VMEM((n_seq, MINE, block), bf16),
                pltpu.VMEM((n_seq, MINE, 2 * block), bf16),
                pltpu.VMEM((n_seq, MINE, block), bf16),
                pltpu.VMEM((n_chan, n_seq, MINE, LANES), bf16),
                pltpu.VMEM((model, LANES), bf16),
                sems((4,)),
                sems((5,)),
            ]
            + [sems((n_seq,))] * 8
            + [sems((n_chan,))] * 2,
            compiler_params=pltpu.CompilerParams(
                collective_id=0, has_side_effects=True, vmem_limit_bytes=48 * 1024 * 1024
            ),
        )(
            values,
            gate_acts,
            cotangent,
            filter_taps,
            jnp.asarray(high),
            jnp.asarray(low),
            w_value,
            w_gate,
        )

    return jax.shard_map(
        local,
        mesh=mesh,
        in_specs=(P("chan", "seq"), P("chan", "seq"), P("chan", "seq"), P("chan", "seq"), P(), P()),
        out_specs=(P(("seq", "chan"), None), P("chan", "seq")),
        check_vma=False,
    )
```

time: 94.9 us -> 64.9 us (0.68)
  Pallas kernels: 0 us -> 55.8 us
  waiting for transfers between devices: 23.8 us -> 0 us
  starting transfers between devices: 23.5 us -> 0 us
  blocking collectives: 15.9 us -> 0 us
  other arithmetic: 10.9 us -> 0 us
  matrix products: 7.09 us -> 0 us
  local copies, waits for them, and re-layouts: 11.9 us -> 8.2 us
    pallas_call x0 -> x1, Pallas kernels: none -> 55.8 us  [local(): pl.pallas_call(functools.partial(kernel, n_seq, n_chan), out_shape=(jax.S...]
    all_to_all x2 -> x0, waiting for transfers between devices: 23.8 us -> none  [the longest x1 14.9 us: local(): got = lax.all_to_all(packed, 'seq', split_axis=0, concat_axis=0, tiled=True)]
    all_to_all x2 -> x0, starting transfers between devices: 23.5 us -> none  [the longest x1 12.4 us: local(): got = lax.all_to_all(packed, 'seq', split_axis=0, concat_axis=0, tiled=True)]
    all_to_all x1 -> x0, blocking collectives: 15.9 us -> none  [local(): back = lax.all_to_all(back, 'seq', split_axis=0, concat_axis=0, tiled=True)]
    dot_general x4 -> x0, matrix products: 7.09 us -> none  [the longest x1 3.2 us: local(): lax.dot_general(got[:, :3], table, (((3,), (0,)), ((), ())), preferred_el...]
    unnamed x40 -> x14, local copies, waits for them, and re-layouts: 3.42 us -> 8.2 us
    concatenate x4 -> x0, other arithmetic: 4.34 us -> none  [local(): jnp.concatenate(t, -1).astype(bf16)]
    add x3 -> x0, other arithmetic: 4.03 us -> none  [the longest x2 2.29 us: corr(): out_i = out_i + (pr[c] * si - pi[c] * sr)]
  transfers between devices with their start and end apart: 2 -> 0, of which waited for: 2 -> 0; matrix products, arithmetic and copies ran while one was open for 1% -> 0% of each run, Pallas kernels for 0% -> 0%
where the time goes in v2:
time: 64.9 us; the launch traced here: 64.7 us
  Pallas kernels  55.8 us (86%)
  local copies, waits for them, and re-layouts  8.2 us (13%)
  between operations  0.65 us (1%)
    pallas_call x1, Pallas kernels, local(): pl.pallas_call(functools.partial(kernel, n_seq, n_chan), out_shape=(jax.S...  55.8 us
    unnamed x14, local copies, waits for them, and re-layouts  8.2 us

profile of v2, /device:TPU:1, one launch (start us, length us, event | category | flops | bytes accessed | tf_op | source)
XLA Modules:
  0.0 64.7 jit_solution(310373494815665044)
XLA Ops:
  0.6 0.0 copy-start
  0.6 1.6 %copy-done = bf16[1024,1024]{1,0:T(8,128)(2,1)S(1)} copy-done((bf16[1024,1024]{1,0:T(8,128)(2,1)S(1)}, bf16[1024,1024]{1,0:T(8,128)(2,1)}, u32[]{:S(2)}) %copy-start) | copy-done | bytes 2097176
  2.2 0.0 copy-start.1
  2.2 1.6 %copy-done.1 = bf16[1024,1024]{1,0:T(8,128)(2,1)S(1)} copy-done((bf16[1024,1024]{1,0:T(8,128)(2,1)S(1)}, bf16[1024,1024]{1,0:T(8,128)(2,1)}, u32[]{:S(2)}) %copy-start.1) | copy-done | bytes 2097176
  3.8 0.0 copy-start.2
  3.8 0.9 %copy-done.2 = f32[64,1024]{1,0:T(8,128)S(1)} copy-done((f32[64,1024]{1,0:T(8,128)S(1)}, f32[64,1024]{1,0:T(8,128)}, u32[]{:S(2)}) %copy-start.2) | copy-done | bytes 262168
  4.8 0.0 copy-start.3
  4.8 0.9 %copy-done.3 = bf16[64,1024]{1,0:T(8,128)(2,1)S(1)} copy-done((bf16[64,1024]{1,0:T(8,128)(2,1)S(1)}, bf16[64,1024]{1,0:T(8,128)(2,1)}, u32[]{:S(2)}) %copy-start.3) | copy-done | bytes 131096
  5.7 0.0 copy-start.4
  5.7 0.9 %copy-done.4 = bf16[64,1024]{1,0:T(8,128)(2,1)S(1)} copy-done((bf16[64,1024]{1,0:T(8,128)(2,1)S(1)}, bf16[64,1024]{1,0:T(8,128)(2,1)}, u32[]{:S(2)}) %copy-start.4) | copy-done | bytes 131096
  6.6 0.0 copy-start.5
  6.6 0.9 %copy-done.5 = bf16[64,1024]{1,0:T(8,128)(2,1)S(1)} copy-done((bf16[64,1024]{1,0:T(8,128)(2,1)S(1)}, bf16[64,1024]{1,0:T(8,128)(2,1)}, u32[]{:S(2)}) %copy-start.5) | copy-done | bytes 131096
  7.5 55.8 %shard_map.95 = (bf16[64,1024]{1,0:T(8,128)(2,1)S(1)}, f32[64,1024]{1,0:T(8,128)S(1)}) custom-call(bf16[64,1024]{1,0:T(8,128)(2,1)S(1)} %copy-done.3, bf16[64,1024]{1,0:T(8,128)(2,1)S(1)} %copy-done.4, bf16[64,1024]{1,0:T(8,128)(2,1)S(1)} %copy-done.5, f32[64,1024]{1,0:T(8,128)S(1)} %copy-done.2, bf16[8,1024,256]{2,1,0:T(8,128)(2,1)} %constant.4.clone.high_hbm, ...), custom_call_target="tpu_custom_call" | custom-call | tf_op jit(solution)/shard_map/pallas_call | solution.py:387
  63.3 0.7 %copy.12 = bf16[64,1024]{1,0:T(8,128)(2,1)} copy(bf16[64,1024]{1,0:T(8,128)(2,1)S(1)} %get-tuple-element.4) | data formatting | bytes 262144
  64.0 0.7 %copy.13 = f32[64,1024]{1,0:T(8,128)} copy(f32[64,1024]{1,0:T(8,128)S(1)} %get-tuple-element.5) | data formatting | bytes 524288
Async XLA Ops:
  0.6 1.6 %copy-start = (bf16[1024,1024]{1,0:T(8,128)(2,1)S(1)}, bf16[1024,1024]{1,0:T(8,128)(2,1)}, u32[]{:S(2)}) copy-start(bf16[1024,1024]{1,0:T(8,128)(2,1)} %wv_hbm.1) | copy-start | bytes 6291460
  2.2 1.6 %copy-start.1 = (bf16[1024,1024]{1,0:T(8,128)(2,1)S(1)}, bf16[1024,1024]{1,0:T(8,128)(2,1)}, u32[]{:S(2)}) copy-start(bf16[1024,1024]{1,0:T(8,128)(2,1)} %wg_hbm.1) | copy-start | bytes 6291460
  3.8 0.9 %copy-start.2 = (f32[64,1024]{1,0:T(8,128)S(1)}, f32[64,1024]{1,0:T(8,128)}, u32[]{:S(2)}) copy-start(f32[64,1024]{1,0:T(8,128)} %taps.1) | copy-start | bytes 786436
  4.8 0.9 %copy-start.3 = (bf16[64,1024]{1,0:T(8,128)(2,1)S(1)}, bf16[64,1024]{1,0:T(8,128)(2,1)}, u32[]{:S(2)}) copy-start(bf16[64,1024]{1,0:T(8,128)(2,1)} %values.1) | copy-start | bytes 393220
  5.7 0.9 %copy-start.4 = (bf16[64,1024]{1,0:T(8,128)(2,1)S(1)}, bf16[64,1024]{1,0:T(8,128)(2,1)}, u32[]{:S(2)}) copy-start(bf16[64,1024]{1,0:T(8,128)(2,1)} %gates.1) | copy-start | bytes 393220
  6.6 0.9 %copy-start.5 = (bf16[64,1024]{1,0:T(8,128)(2,1)S(1)}, bf16[64,1024]{1,0:T(8,128)(2,1)}, u32[]{:S(2)}) copy-start(bf16[64,1024]{1,0:T(8,128)(2,1)} %cotangent.1) | copy-start | bytes 393220

commit v3 on v2

v3 whole, which is shorter than its diff:
```python
import functools

import numpy as np

import jax
import jax.numpy as jnp
import ml_dtypes
from jax import lax
from jax.experimental import pallas as pl
from jax.experimental.pallas import tpu as pltpu
from jax.sharding import PartitionSpec as P

MESH = pl.DeviceIdType.MESH
LANES = 128
MINE = 4


def dft_tables(block):
    chunks = block // LANES
    order = np.concatenate([np.arange(0, block, 2), np.arange(1, block, 2)])
    steps = (2 * order + 1)[None, :] * np.arange(block)[:, None] % (4 * block)
    angle = np.pi * steps / (2 * block)
    table = np.stack([np.cos(angle), -np.sin(angle)]).reshape(2, block, chunks, LANES)
    table = table.transpose(2, 1, 0, 3).reshape(chunks, block, 2 * LANES)
    high = table.astype(ml_dtypes.bfloat16)
    low = (table - high.astype(np.float64)).astype(ml_dtypes.bfloat16)
    return high, low


def kernel(
    n_seq,
    n_chan,
    values_hbm,
    gates_hbm,
    cotangent_hbm,
    taps_hbm,
    high_hbm,
    low_hbm,
    wv_hbm,
    wg_hbm,
    input_grad,
    filter_grad,
    values,
    gates,
    cotangent,
    taps,
    high,
    low,
    wv,
    wg,
    flat,
    send_hv,
    send_u,
    send_c,
    got_hv,
    got_u,
    got_c,
    rows,
    spec,
    swapped,
    doubled,
    prod,
    packed,
    signal,
    send_t,
    send_f,
    got_f,
    tiles,
    stacked,
    load_sem,
    own_sem,
    hv_send,
    hv_recv,
    u_send,
    u_recv,
    c_send,
    c_recv,
    f_send,
    f_recv,
    t_send,
    t_recv,
    met,
):
    f32 = jnp.float32
    bf16 = jnp.bfloat16
    me = lax.axis_index("seq")
    my_chan = lax.axis_index("chan")
    block = values.shape[1]
    chunks = block // LANES
    share = block // n_chan
    pairs = n_seq // 2

    loads = [
        pltpu.make_async_copy(src, dst, load_sem.at[i])
        for i, (src, dst) in enumerate(
            (
                (taps_hbm, taps),
                (values_hbm, values),
                (gates_hbm, gates),
                (cotangent_hbm, cotangent),
                (high_hbm, high),
                (low_hbm, low),
                (wv_hbm, wv),
                (wg_hbm, wg),
            )
        )
    ]
    for load in loads:
        load.start()

    barrier = pltpu.get_barrier_semaphore()

    def greet_seq(k, carry):
        pl.semaphore_signal(
            barrier, inc=1, device_id={"seq": me ^ k}, device_id_type=MESH
        )
        return carry

    def greet_chan(k, carry):
        pl.semaphore_signal(
            barrier, inc=1, device_id={"chan": my_chan ^ k}, device_id_type=MESH
        )
        return carry

    lax.fori_loop(1, n_seq, greet_seq, 0)
    lax.fori_loop(1, n_chan, greet_chan, 0)

    for load in loads[:4]:
        load.wait()
    flat[0] = taps[...]
    flat[1] = values[...].astype(f32)
    cot = cotangent[...].astype(f32)
    flat[2] = cot * gates[...].astype(f32)
    flat[3] = cot

    def pack(t, carry):
        at = pl.ds(pl.multiple_of(t * 8, 8), 8)
        h, v, u, c = (flat[i, at, :] for i in range(4))
        for side in range(2):
            part = slice(side * MINE, side * MINE + MINE)
            hv = jnp.concatenate([h[part], v[part]], 0)
            send_hv[2 * t + side] = hv.astype(bf16)
            send_u[2 * t + side] = u[part].astype(bf16)
            send_c[2 * t + side] = c[part].astype(bf16)
        return carry

    lax.fori_loop(0, pairs, pack, 0)
    pl.semaphore_wait(barrier, n_seq + n_chan - 2)

    def pair_of(i):
        return (me // 2) ^ (2 * (i % (pairs // 2)) + 1 - i // (pairs // 2))

    def to_seq(src, dst, send_sem, recv_sem, peer, slot):
        return pltpu.make_async_remote_copy(
            src_ref=src.at[peer],
            dst_ref=dst.at[slot],
            send_sem=send_sem.at[peer],
            recv_sem=recv_sem.at[slot],
            device_id={"seq": peer},
            device_id_type=MESH,
        )

    def send_all(src, dst, send_sem, recv_sem):
        def step(i, carry):
            for side in range(2):
                peer = 2 * pair_of(i) + side

                @pl.when(peer != me)
                def _():
                    to_seq(src, dst, send_sem, recv_sem, peer, me).start()

            return carry

        lax.fori_loop(0, pairs, step, 0)

    def wait_all(src, dst, send_sem, recv_sem):
        def step(k, carry):
            copy = to_seq(src, dst, send_sem, recv_sem, me ^ k, me ^ k)
            copy.wait_send()
            copy.wait_recv()
            return carry

        lax.fori_loop(1, n_seq, step, 0)

    send_all(send_hv, got_hv, hv_send, hv_recv)
    send_all(send_u, got_u, u_send, u_recv)
    send_all(send_c, got_c, c_send, c_recv)
    own = [
        pltpu.make_async_copy(src.at[me], dst.at[me], own_sem.at[i])
        for i, (src, dst) in enumerate(
            ((send_hv, got_hv), (send_u, got_u), (send_c, got_c))
        )
    ]
    for copy in own:
        copy.start()

    def met_chan(k, carry):
        pl.semaphore_signal(met, inc=1, device_id={"chan": my_chan ^ k}, device_id_type=MESH)
        return carry

    lax.fori_loop(1, n_chan, met_chan, 0)
    loads[4].wait()
    loads[5].wait()
    own[0].wait()
    wait_all(send_hv, got_hv, hv_send, hv_recv)

    def build_hv(t, carry):
        tile = jnp.concatenate([got_hv[2 * t + i].astype(f32) for i in range(2)], 0)
        rows[pl.ds(pl.multiple_of(t * 16, 16), 16), :] = tile.astype(bf16)
        return carry

    lax.fori_loop(0, pairs, build_hv, 0)
    own[1].wait()
    wait_all(send_u, got_u, u_send, u_recv)

    def build_u(t, carry):
        tile = jnp.concatenate([got_u[4 * t + i].astype(f32) for i in range(4)], 0)
        at = pl.ds(pl.multiple_of(n_seq * 8 + t * 16, 16), 16)
        rows[at, :] = tile.astype(bf16)
        return carry

    lax.fori_loop(0, n_seq // 4, build_u, 0)

    re = slice(0, LANES)
    im = slice(LANES, 2 * LANES)
    group = 4
    upper = lax.broadcasted_iota(jnp.int32, (8, LANES), 0) < MINE
    tail = n_seq * 8

    def frequency(j, carry):
        lhs = rows[...]
        spec[...] = jnp.dot(lhs, high[j], preferred_element_type=f32) + jnp.dot(
            lhs, low[j], preferred_element_type=f32
        )
        sign = jnp.where(j < chunks // 2, 1.0, -1.0).astype(f32)

        def first(a):
            at = slice(a * 8, a * 8 + 8)
            return spec[at, re], spec[at, im]

        def second(a):
            at = slice(a * 8, a * 8 + 8)
            return doubled[at, re], doubled[at, im]

        def turned(a):
            at = slice(a * 8, a * 8 + 8)
            return swapped[at, re], swapped[at, im]

        for a in range(n_seq):
            at = slice(a * 8, a * 8 + 8)
            for half in (re, im):
                swapped[at, half] = pltpu.roll(spec[at, half], MINE, axis=0)
        for a in range(0, n_seq, 2):
            for half in (re, im):
                tile = spec[tail + a * 4 : tail + a * 4 + 8, half]
                other = pltpu.roll(tile, MINE, axis=0)
                doubled[a * 8 : a * 8 + 8, half] = jnp.where(upper, tile, other)
                doubled[a * 8 + 8 : a * 8 + 16, half] = jnp.where(upper, other, tile)

        before = None
        for base in range(0, n_seq, group):
            acc = [None] * group
            for x in range((base + group - 1) // 2 + 1):
                pr, pi = first(x)
                for i in range(group):
                    y = base + i - x
                    if y < x:
                        continue
                    qr, qi = turned(y)
                    if y == x:
                        ar, ai = pr * 0.5, pi * 0.5
                    else:
                        ar, ai = pr, pi
                    tr = ar * qr - ai * qi
                    ti = ar * qi + ai * qr
                    acc[i] = (tr, ti) if acc[i] is None else (acc[i][0] + tr, acc[i][1] + ti)
            done = []
            for i in range(group):
                zr, zi = (z + pltpu.roll(z, MINE, axis=0) for z in acc[i])
                if before is None:
                    done.append((zr, zi))
                else:
                    done.append((zr - sign * before[1], zi + sign * before[0]))
                before = (zr, zi)
            for i in range(0, group, 2):
                at = slice(tail + (base + i) * 4, tail + (base + i) * 4 + 8)
                for half, part in ((re, 0), (im, 1)):
                    prod[at, half] = jnp.where(upper, done[i][part], done[i + 1][part])

        after = None
        for base in reversed(range(0, n_seq, group)):
            acc = [None] * group
            for c in range(n_seq - base):
                pr, pi = first(c)
                for i in range(group):
                    if base + i + c >= n_seq:
                        continue
                    qr, qi = second(base + i + c)
                    tr = pr * qr + pi * qi
                    ti = pr * qi - pi * qr
                    acc[i] = (tr, ti) if acc[i] is None else (acc[i][0] + tr, acc[i][1] + ti)
            for i in reversed(range(group)):
                zr, zi = acc[i]
                at = slice((base + i) * 8, (base + i) * 8 + 8)
                if after is None:
                    prod[at, re] = zr
                    prod[at, im] = zi
                else:
                    prod[at, re] = zr + sign * after[1]
                    prod[at, im] = zi - sign * after[0]
                after = (zr, zi)
        packed[j] = prod[...].astype(bf16)
        return carry

    lax.fori_loop(0, chunks, frequency, 0)

    own[2].wait()
    wait_all(send_c, got_c, c_send, c_recv)
    pl.semaphore_wait(met, n_chan - 1)

    wide = 256
    turn = (((1,), (1,)), ((), ()))
    low_lanes = lax.broadcasted_iota(jnp.int32, (MINE, LANES), 1) < share
    per_step = wide // share

    def to_owner(a, c):
        return pltpu.make_async_remote_copy(
            src_ref=send_t.at[a, c],
            dst_ref=tiles.at[my_chan, me],
            send_sem=t_send,
            recv_sem=t_recv,
            device_id={"seq": a, "chan": c},
            device_id_type=MESH,
        )

    def inverse(t, carry):
        at = pl.ds(pl.multiple_of(t * wide, wide), wide)
        total = None
        for j in range(chunks):
            lhs = packed[j]
            part = lax.dot_general(lhs, high[j, at, :], turn, preferred_element_type=f32)
            part = part + lax.dot_general(
                lhs, low[j, at, :], turn, preferred_element_type=f32
            )
            total = part if total is None else total + part
        signal[...] = total * (1.0 / (block * 128.0))

        def finish(i, carry):
            pair = pair_of(i)
            convs = signal[pl.ds(pl.multiple_of(tail + pair * 8, 8), 8), :]
            for side in range(2):
                a = 2 * pair + side
                grads = signal[pl.ds(pl.multiple_of(a * 8, 8), 8), :]
                conv = convs[side * MINE : side * MINE + MINE]
                gate_grad = conv * got_c[a, :, at].astype(f32)
                value_grad = grads[:MINE]
                send_f[a, t] = grads[MINE:].astype(bf16)
                for p in range(wide // LANES):
                    lane = slice(p * LANES, (p + 1) * LANES)
                    x = value_grad[:, lane]
                    y = gate_grad[:, lane]
                    even = jnp.where(low_lanes, x, pltpu.roll(y, share, axis=1))
                    odd = jnp.where(low_lanes, pltpu.roll(x, share, axis=1), y)
                    c = t * per_step + 2 * p
                    send_t[a, c] = even.astype(bf16)
                    send_t[a, c + 1] = odd.astype(bf16)
                for q in range(per_step):
                    c = t * per_step + q

                    @pl.when((a != me) | (c != my_chan))
                    def _():
                        to_owner(a, c).start()

            return carry

        lax.fori_loop(0, pairs, finish, 0)
        return carry

    lax.fori_loop(0, block // wide, inverse, 0)

    own_t = pltpu.make_async_copy(send_t.at[me, my_chan], tiles.at[my_chan, me], t_recv)
    own_f = pltpu.make_async_copy(send_f.at[me], got_f.at[me], own_sem.at[3])
    own_t.start()
    own_f.start()
    send_all(send_f, got_f, f_send, f_recv)
    loads[6].wait()
    loads[7].wait()

    pltpu.make_async_copy(tiles, tiles, t_recv).wait()

    def restack(c, carry):
        for q in range(n_seq // 4):
            tile = jnp.concatenate(
                [tiles[c, 4 * q + i].astype(f32) for i in range(4)], 0
            )
            at = pl.ds(pl.multiple_of(c * 64 + q * 16, 16), 16)
            stacked[at, :] = tile.astype(bf16)
        return carry

    lax.fori_loop(0, n_chan, restack, 0)
    tokens = stacked[...].T
    out = lax.dot_general(tokens[:share], wv[...], turn, preferred_element_type=f32)
    out = out + lax.dot_general(tokens[share:], wg[...], turn, preferred_element_type=f32)
    input_grad[...] = out.astype(bf16)

    own_f.wait()
    wait_all(send_f, got_f, f_send, f_recv)

    def unpack(i, carry):
        at = pl.ds(pl.multiple_of(i * 8, 8), 8)
        for t in range(block // wide):
            pair = [got_f[2 * i + side, t].astype(f32) for side in range(2)]
            filter_grad[at, t * wide : (t + 1) * wide] = jnp.concatenate(pair, 0)
        return carry

    lax.fori_loop(0, pairs, unpack, 0)

    def drain(k, carry):
        pltpu.make_async_copy(send_t.at[k], send_t.at[k], t_send).wait()
        return carry

    lax.fori_loop(1, n_seq, drain, 0)
    rest = send_t.at[0, pl.ds(0, n_chan - 1)]
    pltpu.make_async_copy(rest, rest, t_send).wait()


def solution(mesh):
    n_seq = mesh.shape["seq"]
    n_chan = mesh.shape["chan"]
    bf16 = jnp.bfloat16
    f32 = jnp.float32

    def local(values, gate_acts, cotangent, filter_taps, w_value, w_gate):
        channels, block = values.shape
        chunks = block // LANES
        model = w_value.shape[0]
        high, low = dft_tables(block)
        vmem = pl.BlockSpec(memory_space=pltpu.VMEM)
        hbm = pl.BlockSpec(memory_space=pltpu.MemorySpace.HBM)
        sems = pltpu.SemaphoreType.DMA
        return pl.pallas_call(
            functools.partial(kernel, n_seq, n_chan),
            out_shape=(
                jax.ShapeDtypeStruct((block // n_chan, model), bf16),
                jax.ShapeDtypeStruct((channels, block), f32),
            ),
            in_specs=[hbm] * 8,
            out_specs=(vmem, vmem),
            scratch_shapes=[
                pltpu.VMEM((channels, block), bf16),
                pltpu.VMEM((channels, block), bf16),
                pltpu.VMEM((channels, block), bf16),
                pltpu.VMEM((channels, block), f32),
                pltpu.VMEM((chunks, block, 2 * LANES), bf16),
                pltpu.VMEM((chunks, block, 2 * LANES), bf16),
                pltpu.VMEM((model, model), bf16),
                pltpu.VMEM((model, model), bf16),
                pltpu.VMEM((4, channels, block), f32),
                pltpu.VMEM((n_seq, 2 * MINE, block), bf16),
                pltpu.VMEM((n_seq, MINE, block), bf16),
                pltpu.VMEM((n_seq, MINE, block), bf16),
                pltpu.VMEM((n_seq, 2 * MINE, block), bf16),
                pltpu.VMEM((n_seq, MINE, block), bf16),
                pltpu.VMEM((n_seq, MINE, block), bf16),
                pltpu.VMEM((n_seq * 12, block), bf16),
                pltpu.VMEM((n_seq * 12, 2 * LANES), f32),
                pltpu.VMEM((n_seq * 8, 2 * LANES), f32),
                pltpu.VMEM((n_seq * 8, 2 * LANES), f32),
                pltpu.VMEM((n_seq * 12, 2 * LANES), f32),
                pltpu.VMEM((chunks, n_seq * 12, 2 * LANES), bf16),
                pltpu.VMEM((n_seq * 12, 256), f32),
                pltpu.VMEM((n_seq, n_chan, MINE, LANES), bf16),
                pltpu.VMEM((n_seq, block // 256, MINE, 256), bf16),
                pltpu.VMEM((n_seq, block // 256, MINE, 256), bf16),
                pltpu.VMEM((n_chan, n_seq, MINE, LANES), bf16),
                pltpu.VMEM((model, LANES), bf16),
                sems((8,)),
                sems((4,)),
            ]
            + [sems((n_seq,))] * 8
            + [sems, sems, pltpu.SemaphoreType.REGULAR],
            compiler_params=pltpu.CompilerParams(
                collective_id=0, has_side_effects=True, vmem_limit_bytes=48 * 1024 * 1024
            ),
        )(
            values,
            gate_acts,
            cotangent,
            filter_taps,
            jnp.asarray(high),
            jnp.asarray(low),
            w_value,
            w_gate,
        )

    return jax.shard_map(
        local,
        mesh=mesh,
        in_specs=(P("chan", "seq"), P("chan", "seq"), P("chan", "seq"), P("chan", "seq"), P(), P()),
        out_specs=(P(("seq", "chan"), None), P("chan", "seq")),
        check_vma=False,
    )
```

time: 64.9 us -> 57.9 us (0.89)
  the two profiles are of different devices: /device:TPU:1 before, /device:TPU:33 now
where the time goes in v3:
time: 57.9 us; the launch traced here: 57.6 us
  Pallas kernels  48.8 us (84%)
  local copies, waits for them, and re-layouts  8.2 us (14%)
  between operations  0.65 us (1%)
    pallas_call x1, Pallas kernels, local(): pl.pallas_call(functools.partial(kernel, n_seq, n_chan), out_shape=(jax.S...  48.8 us
    unnamed x14, local copies, waits for them, and re-layouts  8.2 us

profile of v3, /device:TPU:33, one launch (start us, length us, event | category | flops | bytes accessed | tf_op | source)
XLA Modules:
  0.0 57.6 jit_solution(17250644040115783289)
XLA Ops:
  0.6 0.0 copy-start
  0.6 1.6 %copy-done = bf16[1024,1024]{1,0:T(8,128)(2,1)S(1)} copy-done((bf16[1024,1024]{1,0:T(8,128)(2,1)S(1)}, bf16[1024,1024]{1,0:T(8,128)(2,1)}, u32[]{:S(2)}) %copy-start) | copy-done | bytes 2097176
  2.2 0.0 copy-start.1
  2.2 1.6 %copy-done.1 = bf16[1024,1024]{1,0:T(8,128)(2,1)S(1)} copy-done((bf16[1024,1024]{1,0:T(8,128)(2,1)S(1)}, bf16[1024,1024]{1,0:T(8,128)(2,1)}, u32[]{:S(2)}) %copy-start.1) | copy-done | bytes 2097176
  3.8 0.0 copy-start.2
  3.8 0.9 %copy-done.2 = f32[64,1024]{1,0:T(8,128)S(1)} copy-done((f32[64,1024]{1,0:T(8,128)S(1)}, f32[64,1024]{1,0:T(8,128)}, u32[]{:S(2)}) %copy-start.2) | copy-done | bytes 262168
  4.8 0.0 copy-start.3
  4.8 0.9 %copy-done.3 = bf16[64,1024]{1,0:T(8,128)(2,1)S(1)} copy-done((bf16[64,1024]{1,0:T(8,128)(2,1)S(1)}, bf16[64,1024]{1,0:T(8,128)(2,1)}, u32[]{:S(2)}) %copy-start.3) | copy-done | bytes 131096
  5.7 0.0 copy-start.4
  5.7 0.9 %copy-done.4 = bf16[64,1024]{1,0:T(8,128)(2,1)S(1)} copy-done((bf16[64,1024]{1,0:T(8,128)(2,1)S(1)}, bf16[64,1024]{1,0:T(8,128)(2,1)}, u32[]{:S(2)}) %copy-start.4) | copy-done | bytes 131096
  6.6 0.0 copy-start.5
  6.6 0.9 %copy-done.5 = bf16[64,1024]{1,0:T(8,128)(2,1)S(1)} copy-done((bf16[64,1024]{1,0:T(8,128)(2,1)S(1)}, bf16[64,1024]{1,0:T(8,128)(2,1)}, u32[]{:S(2)}) %copy-start.5) | copy-done | bytes 131096
  7.5 48.8 %shard_map.95 = (bf16[64,1024]{1,0:T(8,128)(2,1)S(1)}, f32[64,1024]{1,0:T(8,128)S(1)}) custom-call(bf16[64,1024]{1,0:T(8,128)(2,1)S(1)} %copy-done.3, bf16[64,1024]{1,0:T(8,128)(2,1)S(1)} %copy-done.4, bf16[64,1024]{1,0:T(8,128)(2,1)S(1)} %copy-done.5, f32[64,1024]{1,0:T(8,128)S(1)} %copy-done.2, bf16[8,1024,256]{2,1,0:T(8,128)(2,1)} %constant.4.clone.high_hbm, ...), custom_call_target="tpu_custom_call" | custom-call | tf_op jit(solution)/shard_map/pallas_call | solution.py:441
  56.3 0.7 %copy.12 = bf16[64,1024]{1,0:T(8,128)(2,1)} copy(bf16[64,1024]{1,0:T(8,128)(2,1)S(1)} %get-tuple-element.4) | data formatting | bytes 262144
  56.9 0.7 %copy.13 = f32[64,1024]{1,0:T(8,128)} copy(f32[64,1024]{1,0:T(8,128)S(1)} %get-tuple-element.5) | data formatting | bytes 524288
Async XLA Ops:
  0.6 1.6 %copy-start = (bf16[1024,1024]{1,0:T(8,128)(2,1)S(1)}, bf16[1024,1024]{1,0:T(8,128)(2,1)}, u32[]{:S(2)}) copy-start(bf16[1024,1024]{1,0:T(8,128)(2,1)} %wv_hbm.1) | copy-start | bytes 6291460
  2.2 1.6 %copy-start.1 = (bf16[1024,1024]{1,0:T(8,128)(2,1)S(1)}, bf16[1024,1024]{1,0:T(8,128)(2,1)}, u32[]{:S(2)}) copy-start(bf16[1024,1024]{1,0:T(8,128)(2,1)} %wg_hbm.1) | copy-start | bytes 6291460
  3.8 0.9 %copy-start.2 = (f32[64,1024]{1,0:T(8,128)S(1)}, f32[64,1024]{1,0:T(8,128)}, u32[]{:S(2)}) copy-start(f32[64,1024]{1,0:T(8,128)} %taps_hbm.1) | copy-start | bytes 786436
  4.8 0.9 %copy-start.3 = (bf16[64,1024]{1,0:T(8,128)(2,1)S(1)}, bf16[64,1024]{1,0:T(8,128)(2,1)}, u32[]{:S(2)}) copy-start(bf16[64,1024]{1,0:T(8,128)(2,1)} %values_hbm.1) | copy-start | bytes 393220
  5.7 0.9 %copy-start.4 = (bf16[64,1024]{1,0:T(8,128)(2,1)S(1)}, bf16[64,1024]{1,0:T(8,128)(2,1)}, u32[]{:S(2)}) copy-start(bf16[64,1024]{1,0:T(8,128)(2,1)} %gates_hbm.1) | copy-start | bytes 393220
  6.6 0.9 %copy-start.5 = (bf16[64,1024]{1,0:T(8,128)(2,1)S(1)}, bf16[64,1024]{1,0:T(8,128)(2,1)}, u32[]{:S(2)}) copy-start(bf16[64,1024]{1,0:T(8,128)(2,1)} %cotangent_hbm.1) | copy-start | bytes 393220

commit v4 on v3

v4 whole, which is shorter than its diff:
```python
import functools

import numpy as np

import jax
import jax.numpy as jnp
import ml_dtypes
from jax import lax
from jax.experimental import pallas as pl
from jax.experimental.pallas import tpu as pltpu
from jax.sharding import PartitionSpec as P

MESH = pl.DeviceIdType.MESH
LANES = 128
MINE = 4
GROUP = 4
WIDE = 256


def dft_tables(block):
    half = block // 2
    chunks = half // LANES
    order = np.concatenate([np.arange(0, half, 2), np.arange(1, half, 2)])
    token = np.concatenate([np.arange(0, block, 2), np.arange(1, block, 2)])
    steps = (2 * order + 1)[None, :] * token[:, None] % (4 * block)
    angle = np.pi * steps / (2 * block)
    table = np.stack([np.cos(angle), -np.sin(angle)]).reshape(2, block, chunks, LANES)
    table = table.transpose(2, 1, 0, 3).reshape(chunks, block, 2 * LANES)
    high = table.astype(ml_dtypes.bfloat16)
    low = (table - high.astype(np.float64)).astype(ml_dtypes.bfloat16)
    split = (np.arange(block)[:, None] == token[None, :]).astype(ml_dtypes.bfloat16)
    return high, low, split


def kernel(
    n_seq,
    n_chan,
    values_hbm,
    gates_hbm,
    cotangent_hbm,
    taps_hbm,
    high_hbm,
    low_hbm,
    split_hbm,
    wv_hbm,
    wg_hbm,
    input_grad,
    filter_grad,
    values,
    gates,
    cotangent,
    taps,
    high,
    low,
    split,
    wv,
    wg,
    mixed,
    flat,
    send_uv,
    send_h,
    send_c,
    got_uv,
    got_h,
    got_c,
    rows_uv,
    rows_h,
    spec_uv,
    spec_h,
    sums,
    diffs,
    packed_f,
    packed_m,
    signal_f,
    signal_m,
    send_t,
    send_f,
    got_f,
    tiles,
    stacked,
    load_sem,
    own_sem,
    uv_send,
    uv_recv,
    h_send,
    h_recv,
    c_send,
    c_recv,
    f_send,
    f_recv,
    t_send,
    t_recv,
    met,
):
    f32 = jnp.float32
    bf16 = jnp.bfloat16
    me = lax.axis_index("seq")
    my_chan = lax.axis_index("chan")
    block = values.shape[1]
    half = block // 2
    chunks = half // LANES
    share = block // n_chan
    pairs = n_seq // 2

    loads = [
        pltpu.make_async_copy(src, dst, load_sem.at[i])
        for i, (src, dst) in enumerate(
            (
                (taps_hbm, taps),
                (values_hbm, values),
                (gates_hbm, gates),
                (cotangent_hbm, cotangent),
                (split_hbm, split),
                (high_hbm, high),
                (low_hbm, low),
                (wv_hbm, wv),
                (wg_hbm, wg),
            )
        )
    ]
    for load in loads:
        load.start()

    barrier = pltpu.get_barrier_semaphore()

    def greet_seq(k, carry):
        pl.semaphore_signal(
            barrier, inc=1, device_id={"seq": me ^ k}, device_id_type=MESH
        )
        return carry

    def greet_chan(k, carry):
        pl.semaphore_signal(
            barrier, inc=1, device_id={"chan": my_chan ^ k}, device_id_type=MESH
        )
        return carry

    lax.fori_loop(1, n_seq, greet_seq, 0)
    lax.fori_loop(1, n_chan, greet_chan, 0)

    for load in loads[:4]:
        load.wait()
    channels = values.shape[0]
    mixed[0:channels, :] = taps[...].astype(bf16)
    mixed[channels : 2 * channels, :] = values[...]
    cot = cotangent[...]
    upstream = cot.astype(f32) * gates[...].astype(f32)
    mixed[2 * channels : 3 * channels, :] = upstream.astype(bf16)
    mixed[3 * channels : 4 * channels, :] = cot
    loads[4].wait()

    def divide(t, carry):
        at = pl.ds(pl.multiple_of(t * WIDE, WIDE), WIDE)
        flat[:, at] = jnp.dot(mixed[...], split[:, at], preferred_element_type=f32)
        return carry

    lax.fori_loop(0, block // WIDE, divide, 0)

    def pack(t, carry):
        h, v, u, c = (
            flat[pl.ds(pl.multiple_of(i * channels + t * 8, 8), 8), :] for i in range(4)
        )
        for side in range(2):
            part = slice(side * MINE, side * MINE + MINE)
            uv = jnp.concatenate([u[part], v[part]], 0)
            send_uv[2 * t + side] = uv.astype(bf16)
            send_h[2 * t + side] = h[part].astype(bf16)
            send_c[2 * t + side] = c[part].astype(bf16)
        return carry

    lax.fori_loop(0, pairs, pack, 0)
    pl.semaphore_wait(barrier, n_seq + n_chan - 2)

    def pair_of(i):
        return (me // 2) ^ (2 * (i % (pairs // 2)) + 1 - i // (pairs // 2))

    def to_seq(src, dst, send_sem, recv_sem, peer, slot):
        return pltpu.make_async_remote_copy(
            src_ref=src.at[peer],
            dst_ref=dst.at[slot],
            send_sem=send_sem.at[peer],
            recv_sem=recv_sem.at[slot],
            device_id={"seq": peer},
            device_id_type=MESH,
        )

    def send_all(src, dst, send_sem, recv_sem):
        def step(i, carry):
            for side in range(2):
                peer = 2 * pair_of(i) + side

                @pl.when(peer != me)
                def _():
                    to_seq(src, dst, send_sem, recv_sem, peer, me).start()

            return carry

        lax.fori_loop(0, pairs, step, 0)

    def wait_all(src, dst, send_sem, recv_sem):
        def step(k, carry):
            copy = to_seq(src, dst, send_sem, recv_sem, me ^ k, me ^ k)
            copy.wait_send()
            copy.wait_recv()
            return carry

        lax.fori_loop(1, n_seq, step, 0)

    send_all(send_uv, got_uv, uv_send, uv_recv)
    send_all(send_h, got_h, h_send, h_recv)
    send_all(send_c, got_c, c_send, c_recv)
    own = [
        pltpu.make_async_copy(src.at[me], dst.at[me], own_sem.at[i])
        for i, (src, dst) in enumerate(
            ((send_uv, got_uv), (send_h, got_h), (send_c, got_c))
        )
    ]
    for copy in own:
        copy.start()

    def met_chan(k, carry):
        pl.semaphore_signal(met, inc=1, device_id={"chan": my_chan ^ k}, device_id_type=MESH)
        return carry

    lax.fori_loop(1, n_chan, met_chan, 0)
    loads[5].wait()
    loads[6].wait()
    own[0].wait()
    wait_all(send_uv, got_uv, uv_send, uv_recv)

    flip = jnp.where(
        lax.broadcasted_iota(jnp.int32, (MINE, block), 1) < half, 1.0, -1.0
    ).astype(f32)

    def build_uv(t, carry):
        pair = [got_uv[2 * t + i].astype(f32) for i in range(2)]
        for n, part in enumerate((slice(0, MINE), slice(MINE, 2 * MINE))):
            x, y = pair[0][part], pair[1][part]
            tile = jnp.concatenate([x, x * flip, y, y * flip], 0)
            at = pl.ds(pl.multiple_of(n * n_seq * 8 + t * 16, 16), 16)
            rows_uv[at, :] = tile.astype(bf16)
        return carry

    lax.fori_loop(0, pairs, build_uv, 0)

    re = slice(0, LANES)
    im = slice(LANES, 2 * LANES)
    turn = (((1,), (1,)), ((), ()))
    upper = lax.broadcasted_iota(jnp.int32, (8, LANES), 0) < MINE
    scale = 1.0 / (block * 128.0)

    def times_table(lhs, j):
        return jnp.dot(lhs, high[j], preferred_element_type=f32) + jnp.dot(
            lhs, low[j], preferred_element_type=f32
        )

    def add(acc, term):
        return term if acc is None else (acc[0] + term[0], acc[1] + term[1])

    def fold(base, done, offset):
        for i in range(0, GROUP, 2):
            at = slice(offset + (base + i) * MINE, offset + (base + i) * MINE + 8)
            for lane, part in ((re, 0), (im, 1)):
                x, y = done[i][part], done[i + 1][part]
                rx, ry = pltpu.roll(x, MINE, axis=0), pltpu.roll(y, MINE, axis=0)
                sums[at, lane] = jnp.where(upper, x + rx, y + ry)
                diffs[at, lane] = jnp.where(upper, x - rx, ry - y)

    def correlate(p, q, sign, offset):
        after = None
        for base in reversed(range(0, n_seq, GROUP)):
            acc = [None] * GROUP
            for c in range(n_seq - base):
                pr, pi = p(c)
                for i in range(GROUP):
                    if base + i + c < n_seq:
                        qr, qi = q(base + i + c)
                        acc[i] = add(acc[i], (pr * qr + pi * qi, pr * qi - pi * qr))
            done = [None] * GROUP
            for i in reversed(range(GROUP)):
                zr, zi = acc[i]
                if after is None:
                    done[i] = (zr, zi)
                else:
                    done[i] = (zr + sign * after[1], zi - sign * after[0])
                after = (zr, zi)
            fold(base, done, offset)

    def convolve(p, q, sign, offset):
        before = None
        for base in range(0, n_seq, GROUP):
            acc = [None] * GROUP
            for c in range(base + GROUP):
                pr, pi = p(c)
                for i in range(GROUP):
                    if base + i - c >= 0:
                        qr, qi = q(base + i - c)
                        acc[i] = add(acc[i], (pr * qr - pi * qi, pr * qi + pi * qr))
            done = [None] * GROUP
            for i in range(GROUP):
                zr, zi = acc[i]
                if before is None:
                    done[i] = (zr, zi)
                else:
                    done[i] = (zr - sign * before[1], zi + sign * before[0])
                before = (zr, zi)
            fold(base, done, offset)

    def upstream_of(j):
        def tile(a):
            at = slice(a * 8, a * 8 + 8)
            return spec_uv[j, at, re], spec_uv[j, at, im]

        return tile

    def value_of(j):
        def tile(a):
            at = slice((n_seq + a) * 8, (n_seq + a) * 8 + 8)
            return spec_uv[j, at, re], spec_uv[j, at, im]

        return tile

    def tap(a):
        at = slice(a * 8, a * 8 + 8)
        return spec_h[at, re], spec_h[at, im]

    def sign_of(j):
        return jnp.where(j < chunks // 2, 1.0, -1.0).astype(f32)

    small = n_seq * MINE

    def first_spectra(j, carry):
        spec_uv[j] = times_table(rows_uv[...], j)
        correlate(value_of(j), upstream_of(j), sign_of(j), 0)
        packed_f[0, j] = sums[:small, :].astype(bf16)
        packed_f[1, j] = diffs[:small, :].astype(bf16)
        return carry

    lax.fori_loop(0, chunks, first_spectra, 0)

    def back(packed, parity, start):
        total = None
        at = pl.ds(pl.multiple_of(parity * half + start, WIDE), WIDE)
        for j in range(chunks):
            lhs = packed[parity, j]
            part = lax.dot_general(lhs, high[j, at, :], turn, preferred_element_type=f32)
            part = part + lax.dot_general(
                lhs, low[j, at, :], turn, preferred_element_type=f32
            )
            total = part if total is None else total + part
        return total * scale

    def inverse_f(t, carry):
        for parity in range(2):
            at = pl.ds(pl.multiple_of(parity * half + t * WIDE, WIDE), WIDE)
            signal_f[:, at] = back(packed_f, parity, t * WIDE).astype(bf16)
        return carry

    lax.fori_loop(0, half // WIDE, inverse_f, 0)

    def join(t, carry):
        at = pl.ds(pl.multiple_of(t * WIDE, WIDE), WIDE)
        whole = lax.dot_general(
            signal_f[...], split[at, :], turn, preferred_element_type=f32
        )
        for a in range(n_seq):
            send_f[a, t] = whole[a * MINE : a * MINE + MINE].astype(bf16)
        return carry

    lax.fori_loop(0, block // WIDE, join, 0)
    own_f = pltpu.make_async_copy(send_f.at[me], got_f.at[me], own_sem.at[3])
    own_f.start()
    send_all(send_f, got_f, f_send, f_recv)

    own[1].wait()
    wait_all(send_h, got_h, h_send, h_recv)

    def build_h(t, carry):
        x, y = (got_h[2 * t + i].astype(f32) for i in range(2))
        tile = jnp.concatenate([x, x * flip, y, y * flip], 0)
        rows_h[pl.ds(pl.multiple_of(t * 16, 16), 16), :] = tile.astype(bf16)
        return carry

    lax.fori_loop(0, pairs, build_h, 0)

    def second_spectra(j, carry):
        spec_h[...] = times_table(rows_h[...], j)
        correlate(tap, upstream_of(j), sign_of(j), 0)
        convolve(tap, value_of(j), sign_of(j), small)
        packed_m[0, j] = sums[...].astype(bf16)
        packed_m[1, j] = diffs[...].astype(bf16)
        return carry

    lax.fori_loop(0, chunks, second_spectra, 0)

    own[2].wait()
    wait_all(send_c, got_c, c_send, c_recv)
    pl.semaphore_wait(met, n_chan - 1)

    piece = share // 2
    lane_piece = lax.broadcasted_iota(jnp.int32, (8, LANES), 1) // piece
    per_tile = LANES // piece

    def to_owner(a, c):
        return pltpu.make_async_remote_copy(
            src_ref=send_t.at[a, c],
            dst_ref=tiles.at[my_chan, me],
            send_sem=t_send,
            recv_sem=t_recv,
            device_id={"seq": a, "chan": c},
            device_id_type=MESH,
        )

    def inverse_m(t, carry):
        for parity in range(2):
            signal_m[parity] = back(packed_m, parity, t * WIDE)

        def finish(i, carry):
            pair = pair_of(i)
            at_v = pl.ds(pl.multiple_of(pair * 8, 8), 8)
            at_c = pl.ds(pl.multiple_of(small + pair * 8, 8), 8)
            parts = [signal_m[parity, at_v, :] for parity in range(2)]
            for parity in range(2):
                at = pl.ds(pl.multiple_of(parity * half + t * WIDE, WIDE), WIDE)
                cots = jnp.concatenate(
                    [got_c[2 * pair + side, :, at].astype(f32) for side in range(2)], 0
                )
                parts.append(signal_m[parity, at_c, :] * cots)
            for p in range(WIDE // LANES):
                lane = slice(p * LANES, (p + 1) * LANES)
                moved = [parts[0][:, lane]] + [
                    pltpu.roll(parts[n][:, lane], n * piece, axis=1) for n in range(1, 4)
                ]
                for q in range(per_tile):
                    out = moved[0]
                    for n in range(1, 4):
                        out = jnp.where(lane_piece == (q + n) % 4, moved[n], out)
                    c = (t * (WIDE // LANES) + p) * per_tile + q
                    for side in range(2):
                        part = out[side * MINE : side * MINE + MINE]
                        send_t[2 * pair + side, c] = part.astype(bf16)
            for q in range(WIDE // piece):
                c = t * (WIDE // piece) + q
                for side in range(2):
                    a = 2 * pair + side

                    @pl.when((a != me) | (c != my_chan))
                    def _():
                        to_owner(a, c).start()

            return carry

        lax.fori_loop(0, pairs, finish, 0)
        return carry

    lax.fori_loop(0, half // WIDE, inverse_m, 0)
    own_t = pltpu.make_async_copy(send_t.at[me, my_chan], tiles.at[my_chan, me], t_recv)
    own_t.start()

    own_f.wait()
    wait_all(send_f, got_f, f_send, f_recv)

    def unpack(i, carry):
        at = pl.ds(pl.multiple_of(i * 8, 8), 8)
        for t in range(block // WIDE):
            pair = [got_f[2 * i + side, t].astype(f32) for side in range(2)]
            filter_grad[at, t * WIDE : (t + 1) * WIDE] = jnp.concatenate(pair, 0)
        return carry

    lax.fori_loop(0, pairs, unpack, 0)
    loads[7].wait()
    loads[8].wait()

    pltpu.make_async_copy(tiles, tiles, t_recv).wait()

    def restack(c, carry):
        for q in range(n_seq // 4):
            tile = jnp.concatenate(
                [tiles[c, 4 * q + i].astype(f32) for i in range(4)], 0
            )
            at = pl.ds(pl.multiple_of(c * 64 + q * 16, 16), 16)
            stacked[at, :] = tile.astype(bf16)
        return carry

    lax.fori_loop(0, n_chan, restack, 0)

    lane_of = lax.broadcasted_iota(jnp.int32, (LANES, LANES), 1)
    row_of = lax.broadcasted_iota(jnp.int32, (LANES, LANES), 0)
    source = (lane_of // piece + 4 - my_chan % 4) % 4
    wanted = (source // 2) * share + 2 * (lane_of % piece) + source % 2
    choice = jnp.where(row_of == wanted, 1.0, 0.0).astype(bf16)
    tokens = lax.dot_general(choice, stacked[...], turn, preferred_element_type=f32)
    tokens = tokens.astype(bf16)
    out = lax.dot_general(tokens[:share], wv[...], turn, preferred_element_type=f32)
    out = out + lax.dot_general(tokens[share:], wg[...], turn, preferred_element_type=f32)
    input_grad[...] = out.astype(bf16)

    def drain(k, carry):
        pltpu.make_async_copy(send_t.at[k], send_t.at[k], t_send).wait()
        return carry

    lax.fori_loop(1, n_seq, drain, 0)
    rest = send_t.at[0, pl.ds(0, n_chan - 1)]
    pltpu.make_async_copy(rest, rest, t_send).wait()


def solution(mesh):
    n_seq = mesh.shape["seq"]
    n_chan = mesh.shape["chan"]
    bf16 = jnp.bfloat16
    f32 = jnp.float32

    def local(values, gate_acts, cotangent, filter_taps, w_value, w_gate):
        channels, block = values.shape
        chunks = block // 2 // LANES
        model = w_value.shape[0]
        high, low, split = dft_tables(block)
        vmem = pl.BlockSpec(memory_space=pltpu.VMEM)
        hbm = pl.BlockSpec(memory_space=pltpu.MemorySpace.HBM)
        sems = pltpu.SemaphoreType.DMA
        return pl.pallas_call(
            functools.partial(kernel, n_seq, n_chan),
            out_shape=(
                jax.ShapeDtypeStruct((block // n_chan, model), bf16),
                jax.ShapeDtypeStruct((channels, block), f32),
            ),
            in_specs=[hbm] * 9,
            out_specs=(vmem, vmem),
            scratch_shapes=[
                pltpu.VMEM((channels, block), bf16),
                pltpu.VMEM((channels, block), bf16),
                pltpu.VMEM((channels, block), bf16),
                pltpu.VMEM((channels, block), f32),
                pltpu.VMEM((chunks, block, 2 * LANES), bf16),
                pltpu.VMEM((chunks, block, 2 * LANES), bf16),
                pltpu.VMEM((block, block), bf16),
                pltpu.VMEM((model, model), bf16),
                pltpu.VMEM((model, model), bf16),
                pltpu.VMEM((4 * channels, block), bf16),
                pltpu.VMEM((4 * channels, block), f32),
                pltpu.VMEM((n_seq, 2 * MINE, block), bf16),
                pltpu.VMEM((n_seq, MINE, block), bf16),
                pltpu.VMEM((n_seq, MINE, block), bf16),
                pltpu.VMEM((n_seq, 2 * MINE, block), bf16),
                pltpu.VMEM((n_seq, MINE, block), bf16),
                pltpu.VMEM((n_seq, MINE, block), bf16),
                pltpu.VMEM((n_seq * 16, block), bf16),
                pltpu.VMEM((n_seq * 8, block), bf16),
                pltpu.VMEM((chunks, n_seq * 16, 2 * LANES), f32),
                pltpu.VMEM((n_seq * 8, 2 * LANES), f32),
                pltpu.VMEM((n_seq * 8, 2 * LANES), f32),
                pltpu.VMEM((n_seq * 8, 2 * LANES), f32),
                pltpu.VMEM((2, chunks, n_seq * 4, 2 * LANES), bf16),
                pltpu.VMEM((2, chunks, n_seq * 8, 2 * LANES), bf16),
                pltpu.VMEM((n_seq * 4, block), bf16),
                pltpu.VMEM((2, n_seq * 8, WIDE), f32),
                pltpu.VMEM((n_seq, n_chan, MINE, LANES), bf16),
                pltpu.VMEM((n_seq, block // WIDE, MINE, WIDE), bf16),
                pltpu.VMEM((n_seq, block // WIDE, MINE, WIDE), bf16),
                pltpu.VMEM((n_chan, n_seq, MINE, LANES), bf16),
                pltpu.VMEM((model, LANES), bf16),
                sems((9,)),
                sems((4,)),
            ]
            + [sems((n_seq,))] * 8
            + [sems, sems, pltpu.SemaphoreType.REGULAR],
            compiler_params=pltpu.CompilerParams(
                collective_id=0, has_side_effects=True, vmem_limit_bytes=67_043_328
            ),
        )(
            values,
            gate_acts,
            cotangent,
            filter_taps,
            jnp.asarray(high),
            jnp.asarray(low),
            jnp.asarray(split),
            w_value,
            w_gate,
        )

    return jax.shard_map(
        local,
        mesh=mesh,
        in_specs=(P("chan", "seq"), P("chan", "seq"), P("chan", "seq"), P("chan", "seq"), P(), P()),
        out_specs=(P(("seq", "chan"), None), P("chan", "seq")),
        check_vma=False,
    )
```

time: 57.9 us -> 50.8 us (0.88)
  the two profiles are of different devices: /device:TPU:33 before, /device:TPU:1 now
where the time goes in v4:
time: 50.8 us; the launch traced here: 50.7 us
  Pallas kernels  46.8 us (92%)
  local copies, waits for them, and re-layouts  3.24 us (6%)
  between operations  0.64 us (1%)
    pallas_call x1, Pallas kernels, local(): pl.pallas_call(functools.partial(kernel, n_seq, n_chan), out_shape=(jax.S...  46.8 us
    unnamed x2, local copies, waits for them, and re-layouts  3.24 us

profile of v4, /device:TPU:1, one launch (start us, length us, event | category | flops | bytes accessed | tf_op | source)
XLA Modules:
  0.0 50.7 jit_solution(1387759118040896828)
XLA Ops:
  0.6 46.8 %shard_map.104 = (bf16[64,1024]{1,0:T(8,128)(2,1)}, f32[64,1024]{1,0:T(8,128)}) custom-call(bf16[64,1024]{1,0:T(8,128)(2,1)} %values_hbm.1, bf16[64,1024]{1,0:T(8,128)(2,1)} %gates_hbm.1, bf16[64,1024]{1,0:T(8,128)(2,1)} %cotangent_hbm.1, f32[64,1024]{1,0:T(8,128)} %taps_hbm.1, bf16[4,1024,256]{2,1,0:T(8,128)(2,1)} %constant.6.clone.high_hbm, ...), custom_call_target="tpu_custom_call" | custom-call | tf_op jit(solution)/shard_map/pallas_call | solution.py:521
  47.5 1.6 %copy.13 = bf16[64,1024]{1,0:T(8,128)(2,1)} copy(bf16[64,1024]{1,0:T(8,128)(2,1)} %get-tuple-element.4) | data formatting | bytes 262144
  49.0 1.7 %copy.14 = f32[64,1024]{1,0:T(8,128)} copy(f32[64,1024]{1,0:T(8,128)} %get-tuple-element.5) | data formatting | bytes 524288

commit v5 on v4

--- a/solution.py
+++ b/solution.py
@@ -257,16 +257,16 @@
     def add(acc, term):
         return term if acc is None else (acc[0] + term[0], acc[1] + term[1])
 
-    def fold(base, done, offset):
+    def fold(base, done, j, offset):
         for i in range(0, GROUP, 2):
             at = slice(offset + (base + i) * MINE, offset + (base + i) * MINE + 8)
             for lane, part in ((re, 0), (im, 1)):
                 x, y = done[i][part], done[i + 1][part]
                 rx, ry = pltpu.roll(x, MINE, axis=0), pltpu.roll(y, MINE, axis=0)
-                sums[at, lane] = jnp.where(upper, x + rx, y + ry)
-                diffs[at, lane] = jnp.where(upper, x - rx, ry - y)
-
-    def correlate(p, q, sign, offset):
+                sums[j, at, lane] = jnp.where(upper, x + rx, y + ry)
+                diffs[j, at, lane] = jnp.where(upper, x - rx, ry - y)
+
+    def correlate(p, q, sign, j, offset):
         after = None
         for base in reversed(range(0, n_seq, GROUP)):
             acc = [None] * GROUP
@@ -284,9 +284,9 @@
                 else:
                     done[i] = (zr + sign * after[1], zi - sign * after[0])
                 after = (zr, zi)
-            fold(base, done, offset)
-
-    def convolve(p, q, sign, offset):
+            fold(base, done, j, offset)
+
+    def convolve(p, q, sign, j, offset):
         before = None
         for base in range(0, n_seq, GROUP):
             acc = [None] * GROUP
@@ -304,7 +304,7 @@
                 else:
                     done[i] = (zr - sign * before[1], zi + sign * before[0])
                 before = (zr, zi)
-            fold(base, done, offset)
+            fold(base, done, j, offset)
 
     def upstream_of(j):
         def tile(a):
@@ -320,9 +320,12 @@
 
         return tile
 
-    def tap(a):
-        at = slice(a * 8, a * 8 + 8)
-        return spec_h[at, re], spec_h[at, im]
+    def tap_of(j):
+        def tile(a):
+            at = slice(a * 8, a * 8 + 8)
+            return spec_h[j, at, re], spec_h[j, at, im]
+
+        return tile
 
     def sign_of(j):
         return jnp.where(j < chunks // 2, 1.0, -1.0).astype(f32)
@@ -331,43 +334,34 @@
 
     def first_spectra(j, carry):
         spec_uv[j] = times_table(rows_uv[...], j)
-        correlate(value_of(j), upstream_of(j), sign_of(j), 0)
-        packed_f[0, j] = sums[:small, :].astype(bf16)
-        packed_f[1, j] = diffs[:small, :].astype(bf16)
+        correlate(value_of(j), upstream_of(j), sign_of(j), j, 0)
+        packed_f[0, j] = sums[j, :small, :].astype(bf16)
+        packed_f[1, j] = diffs[j, :small, :].astype(bf16)
         return carry
 
     lax.fori_loop(0, chunks, first_spectra, 0)
 
-    def back(packed, parity, start):
+    def back(packed, parity, start, tables):
         total = None
         at = pl.ds(pl.multiple_of(parity * half + start, WIDE), WIDE)
         for j in range(chunks):
             lhs = packed[parity, j]
-            part = lax.dot_general(lhs, high[j, at, :], turn, preferred_element_type=f32)
-            part = part + lax.dot_general(
-                lhs, low[j, at, :], turn, preferred_element_type=f32
-            )
-            total = part if total is None else total + part
+            for table in tables:
+                part = lax.dot_general(
+                    lhs, table[j, at, :], turn, preferred_element_type=f32
+                )
+                total = part if total is None else total + part
         return total * scale
 
     def inverse_f(t, carry):
         for parity in range(2):
-            at = pl.ds(pl.multiple_of(parity * half + t * WIDE, WIDE), WIDE)
-            signal_f[:, at] = back(packed_f, parity, t * WIDE).astype(bf16)
+            grads = back(packed_f, parity, t * WIDE, (high,))
+            for a in range(n_seq):
+                part = grads[a * MINE : a * MINE + MINE]
+                send_f[a, parity * (half // WIDE) + t] = part.astype(bf16)
         return carry
 
     lax.fori_loop(0, half // WIDE, inverse_f, 0)
-
-    def join(t, carry):
-        at = pl.ds(pl.multiple_of(t * WIDE, WIDE), WIDE)
-        whole = lax.dot_general(
-            signal_f[...], split[at, :], turn, preferred_element_type=f32
-        )
-        for a in range(n_seq):
-            send_f[a, t] = whole[a * MINE : a * MINE + MINE].astype(bf16)
-        return carry
-
-    lax.fori_loop(0, block // WIDE, join, 0)
     own_f = pltpu.make_async_copy(send_f.at[me], got_f.at[me], own_sem.at[3])
     own_f.start()
     send_all(send_f, got_f, f_send, f_recv)
@@ -383,15 +377,14 @@
 
     lax.fori_loop(0, pairs, build_h, 0)
 
-    def second_spectra(j, carry):
-        spec_h[...] = times_table(rows_h[...], j)
-        correlate(tap, upstream_of(j), sign_of(j), 0)
-        convolve(tap, value_of(j), sign_of(j), small)
-        packed_m[0, j] = sums[...].astype(bf16)
-        packed_m[1, j] = diffs[...].astype(bf16)
-        return carry
-
-    lax.fori_loop(0, chunks, second_spectra, 0)
+    spec_h[0] = times_table(rows_h[...], 0)
+    for j in range(chunks):
+        if j + 1 < chunks:
+            spec_h[j + 1] = times_table(rows_h[...], j + 1)
+        correlate(tap_of(j), upstream_of(j), 1.0 if j < chunks // 2 else -1.0, j, 0)
+        convolve(tap_of(j), value_of(j), 1.0 if j < chunks // 2 else -1.0, j, small)
+        packed_m[0, j] = sums[j].astype(bf16)
+        packed_m[1, j] = diffs[j].astype(bf16)
 
     own[2].wait()
     wait_all(send_c, got_c, c_send, c_recv)
@@ -413,7 +406,7 @@
 
     def inverse_m(t, carry):
         for parity in range(2):
-            signal_m[parity] = back(packed_m, parity, t * WIDE)
+            signal_m[parity] = back(packed_m, parity, t * WIDE, (high, low))
 
         def finish(i, carry):
             pair = pair_of(i)
@@ -461,13 +454,23 @@
     wait_all(send_f, got_f, f_send, f_recv)
 
     def unpack(i, carry):
-        at = pl.ds(pl.multiple_of(i * 8, 8), 8)
+        at = pl.ds(pl.multiple_of(i * 16, 16), 16)
         for t in range(block // WIDE):
-            pair = [got_f[2 * i + side, t].astype(f32) for side in range(2)]
-            filter_grad[at, t * WIDE : (t + 1) * WIDE] = jnp.concatenate(pair, 0)
-        return carry
-
-    lax.fori_loop(0, pairs, unpack, 0)
+            tile = [got_f[4 * i + n, t].astype(f32) for n in range(4)]
+            lane = slice(t * WIDE, (t + 1) * WIDE)
+            signal_f[at, lane] = jnp.concatenate(tile, 0).astype(bf16)
+        return carry
+
+    lax.fori_loop(0, n_seq // 4, unpack, 0)
+
+    def join(t, carry):
+        at = pl.ds(pl.multiple_of(t * WIDE, WIDE), WIDE)
+        filter_grad[:, at] = lax.dot_general(
+            signal_f[...], split[at, :], turn, preferred_element_type=f32
+        )
+        return carry
+
+    lax.fori_loop(0, block // WIDE, join, 0)
     loads[7].wait()
     loads[8].wait()
 
@@ -547,9 +550,9 @@
                 pltpu.VMEM((n_seq * 16, block), bf16),
                 pltpu.VMEM((n_seq * 8, block), bf16),
                 pltpu.VMEM((chunks, n_seq * 16, 2 * LANES), f32),
-                pltpu.VMEM((n_seq * 8, 2 * LANES), f32),
-                pltpu.VMEM((n_seq * 8, 2 * LANES), f32),
-                pltpu.VMEM((n_seq * 8, 2 * LANES), f32),
+                pltpu.VMEM((chunks, n_seq * 8, 2 * LANES), f32),
+                pltpu.VMEM((chunks, n_seq * 8, 2 * LANES), f32),
+                pltpu.VMEM((chunks, n_seq * 8, 2 * LANES), f32),
                 pltpu.VMEM((2, chunks, n_seq * 4, 2 * LANES), bf16),
                 pltpu.VMEM((2, chunks, n_seq * 8, 2 * LANES), bf16),
                 pltpu.VMEM((n_seq * 4, block), bf16),

time: 50.8 us -> 48.8 us (0.961)
  Pallas kernels: 46.8 us -> 44.8 us
    pallas_call x1, Pallas kernels: 46.8 us -> 44.8 us  [local(): pl.pallas_call(functools.partial(kernel, n_seq, n_chan), out_shape=(jax.S...]
where the time goes in v5:
time: 48.8 us; the launch traced here: 48.7 us
  Pallas kernels  44.8 us (92%)
  local copies, waits for them, and re-layouts  3.24 us (7%)
  between operations  0.64 us (1%)
    pallas_call x1, Pallas kernels, local(): pl.pallas_call(functools.partial(kernel, n_seq, n_chan), out_shape=(jax.S...  44.8 us
    unnamed x2, local copies, waits for them, and re-layouts  3.24 us

profile of v5, /device:TPU:1, one launch (start us, length us, event | category | flops | bytes accessed | tf_op | source)
XLA Modules:
  0.0 48.7 jit_solution(12549455409893199786)
XLA Ops:
  0.6 44.8 %shard_map.104 = (bf16[64,1024]{1,0:T(8,128)(2,1)}, f32[64,1024]{1,0:T(8,128)}) custom-call(bf16[64,1024]{1,0:T(8,128)(2,1)} %values_hbm.1, bf16[64,1024]{1,0:T(8,128)(2,1)} %gates_hbm.1, bf16[64,1024]{1,0:T(8,128)(2,1)} %cotangent_hbm.1, f32[64,1024]{1,0:T(8,128)} %taps_hbm.1, bf16[4,1024,256]{2,1,0:T(8,128)(2,1)} %constant.6.clone.high_hbm, ...), custom_call_target="tpu_custom_call" | custom-call | tf_op jit(solution)/shard_map/pallas_call | solution.py:524
  45.4 1.6 %copy.13 = bf16[64,1024]{1,0:T(8,128)(2,1)} copy(bf16[64,1024]{1,0:T(8,128)(2,1)} %get-tuple-element.4) | data formatting | bytes 262144
  47.0 1.7 %copy.14 = f32[64,1024]{1,0:T(8,128)} copy(f32[64,1024]{1,0:T(8,128)} %get-tuple-element.5) | data formatting | bytes 524288

commit v6 on v5

--- a/solution.py
+++ b/solution.py
@@ -57,15 +57,19 @@
     wg,
     mixed,
     flat,
-    send_uv,
+    send_u,
+    send_v,
     send_h,
     send_c,
-    got_uv,
+    got_u,
+    got_v,
     got_h,
     got_c,
-    rows_uv,
+    rows_u,
+    rows_v,
     rows_h,
-    spec_uv,
+    spec_u,
+    spec_v,
     spec_h,
     sums,
     diffs,
@@ -80,8 +84,10 @@
     stacked,
     load_sem,
     own_sem,
-    uv_send,
-    uv_recv,
+    u_send,
+    u_recv,
+    v_send,
+    v_recv,
     h_send,
     h_recv,
     c_send,
@@ -135,7 +141,8 @@
         )
         return carry
 
-    lax.fori_loop(1, n_seq, greet_seq, 0)
+    for k in sorted(range(1, n_seq), key=lambda k: -(k & 2)):
+        greet_seq(k, 0)
     lax.fori_loop(1, n_chan, greet_chan, 0)
 
     for load in loads[:4]:
@@ -162,8 +169,8 @@
         )
         for side in range(2):
             part = slice(side * MINE, side * MINE + MINE)
-            uv = jnp.concatenate([u[part], v[part]], 0)
-            send_uv[2 * t + side] = uv.astype(bf16)
+            send_u[2 * t + side] = u[part].astype(bf16)
+            send_v[2 * t + side] = v[part].astype(bf16)
             send_h[2 * t + side] = h[part].astype(bf16)
             send_c[2 * t + side] = c[part].astype(bf16)
         return carry
@@ -206,13 +213,14 @@
 
         lax.fori_loop(1, n_seq, step, 0)
 
-    send_all(send_uv, got_uv, uv_send, uv_recv)
+    send_all(send_u, got_u, u_send, u_recv)
+    send_all(send_v, got_v, v_send, v_recv)
     send_all(send_h, got_h, h_send, h_recv)
     send_all(send_c, got_c, c_send, c_recv)
     own = [
         pltpu.make_async_copy(src.at[me], dst.at[me], own_sem.at[i])
         for i, (src, dst) in enumerate(
-            ((send_uv, got_uv), (send_h, got_h), (send_c, got_c))
+            ((send_u, got_u), (send_h, got_h), (send_c, got_c), (send_v, got_v))
         )
     ]
     for copy in own:
@@ -225,23 +233,18 @@
     lax.fori_loop(1, n_chan, met_chan, 0)
     loads[5].wait()
     loads[6].wait()
-    own[0].wait()
-    wait_all(send_uv, got_uv, uv_send, uv_recv)
-
     flip = jnp.where(
         lax.broadcasted_iota(jnp.int32, (MINE, block), 1) < half, 1.0, -1.0
     ).astype(f32)
 
-    def build_uv(t, carry):
-        pair = [got_uv[2 * t + i].astype(f32) for i in range(2)]
-        for n, part in enumerate((slice(0, MINE), slice(MINE, 2 * MINE))):
-            x, y = pair[0][part], pair[1][part]
+    def build(got, rows):
+        def step(t, carry):
+            x, y = (got[2 * t + i].astype(f32) for i in range(2))
             tile = jnp.concatenate([x, x * flip, y, y * flip], 0)
-            at = pl.ds(pl.multiple_of(n * n_seq * 8 + t * 16, 16), 16)
-            rows_uv[at, :] = tile.astype(bf16)
-        return carry
-
-    lax.fori_loop(0, pairs, build_uv, 0)
+            rows[pl.ds(pl.multiple_of(t * 16, 16), 16), :] = tile.astype(bf16)
+            return carry
+
+        lax.fori_loop(0, pairs, step, 0)
 
     re = slice(0, LANES)
     im = slice(LANES, 2 * LANES)
@@ -306,40 +309,35 @@
                 before = (zr, zi)
             fold(base, done, j, offset)
 
-    def upstream_of(j):
+    def tiles_of(spectra, j):
         def tile(a):
             at = slice(a * 8, a * 8 + 8)
-            return spec_uv[j, at, re], spec_uv[j, at, im]
+            return spectra[j, at, re], spectra[j, at, im]
 
         return tile
 
-    def value_of(j):
-        def tile(a):
-            at = slice((n_seq + a) * 8, (n_seq + a) * 8 + 8)
-            return spec_uv[j, at, re], spec_uv[j, at, im]
-
-        return tile
-
-    def tap_of(j):
-        def tile(a):
-            at = slice(a * 8, a * 8 + 8)
-            return spec_h[j, at, re], spec_h[j, at, im]
-
-        return tile
-
-    def sign_of(j):
-        return jnp.where(j < chunks // 2, 1.0, -1.0).astype(f32)
-
     small = n_seq * MINE
 
-    def first_spectra(j, carry):
-        spec_uv[j] = times_table(rows_uv[...], j)
-        correlate(value_of(j), upstream_of(j), sign_of(j), j, 0)
+    own[0].wait()
+    wait_all(send_u, got_u, u_send, u_recv)
+    build(got_u, rows_u)
+
+    def upstream_spectra(j, carry):
+        spec_u[j] = times_table(rows_u[...], j)
+        return carry
+
+    lax.fori_loop(0, chunks, upstream_spectra, 0)
+    own[3].wait()
+    wait_all(send_v, got_v, v_send, v_recv)
+    build(got_v, rows_v)
+    spec_v[0] = times_table(rows_v[...], 0)
+    for j in range(chunks):
+        if j + 1 < chunks:
+            spec_v[j + 1] = times_table(rows_v[...], j + 1)
+        sign = 1.0 if j < chunks // 2 else -1.0
+        correlate(tiles_of(spec_v, j), tiles_of(spec_u, j), sign, j, 0)
         packed_f[0, j] = sums[j, :small, :].astype(bf16)
         packed_f[1, j] = diffs[j, :small, :].astype(bf16)
-        return carry
-
-    lax.fori_loop(0, chunks, first_spectra, 0)
 
     def back(packed, parity, start, tables):
         total = None
@@ -362,27 +360,21 @@
         return carry
 
     lax.fori_loop(0, half // WIDE, inverse_f, 0)
-    own_f = pltpu.make_async_copy(send_f.at[me], got_f.at[me], own_sem.at[3])
+    own_f = pltpu.make_async_copy(send_f.at[me], got_f.at[me], own_sem.at[4])
     own_f.start()
     send_all(send_f, got_f, f_send, f_recv)
 
     own[1].wait()
     wait_all(send_h, got_h, h_send, h_recv)
 
-    def build_h(t, carry):
-        x, y = (got_h[2 * t + i].astype(f32) for i in range(2))
-        tile = jnp.concatenate([x, x * flip, y, y * flip], 0)
-        rows_h[pl.ds(pl.multiple_of(t * 16, 16), 16), :] = tile.astype(bf16)
-        return carry
-
-    lax.fori_loop(0, pairs, build_h, 0)
-
+    build(got_h, rows_h)
     spec_h[0] = times_table(rows_h[...], 0)
     for j in range(chunks):
         if j + 1 < chunks:
             spec_h[j + 1] = times_table(rows_h[...], j + 1)
-        correlate(tap_of(j), upstream_of(j), 1.0 if j < chunks // 2 else -1.0, j, 0)
-        convolve(tap_of(j), value_of(j), 1.0 if j < chunks // 2 else -1.0, j, small)
+        sign = 1.0 if j < chunks // 2 else -1.0
+        correlate(tiles_of(spec_h, j), tiles_of(spec_u, j), sign, j, 0)
+        convolve(tiles_of(spec_h, j), tiles_of(spec_v, j), sign, j, small)
         packed_m[0, j] = sums[j].astype(bf16)
         packed_m[1, j] = diffs[j].astype(bf16)
 
@@ -541,15 +533,19 @@
                 pltpu.VMEM((model, model), bf16),
                 pltpu.VMEM((4 * channels, block), bf16),
                 pltpu.VMEM((4 * channels, block), f32),
-                pltpu.VMEM((n_seq, 2 * MINE, block), bf16),
-                pltpu.VMEM((n_seq, MINE, block), bf16),
-                pltpu.VMEM((n_seq, MINE, block), bf16),
-                pltpu.VMEM((n_seq, 2 * MINE, block), bf16),
-                pltpu.VMEM((n_seq, MINE, block), bf16),
-                pltpu.VMEM((n_seq, MINE, block), bf16),
-                pltpu.VMEM((n_seq * 16, block), bf16),
+                pltpu.VMEM((n_seq, MINE, block), bf16),
+                pltpu.VMEM((n_seq, MINE, block), bf16),
+                pltpu.VMEM((n_seq, MINE, block), bf16),
+                pltpu.VMEM((n_seq, MINE, block), bf16),
+                pltpu.VMEM((n_seq, MINE, block), bf16),
+                pltpu.VMEM((n_seq, MINE, block), bf16),
+                pltpu.VMEM((n_seq, MINE, block), bf16),
+                pltpu.VMEM((n_seq, MINE, block), bf16),
                 pltpu.VMEM((n_seq * 8, block), bf16),
-                pltpu.VMEM((chunks, n_seq * 16, 2 * LANES), f32),
+                pltpu.VMEM((n_seq * 8, block), bf16),
+                pltpu.VMEM((n_seq * 8, block), bf16),
+                pltpu.VMEM((chunks, n_seq * 8, 2 * LANES), f32),
+                pltpu.VMEM((chunks, n_seq * 8, 2 * LANES), f32),
                 pltpu.VMEM((chunks, n_seq * 8, 2 * LANES), f32),
                 pltpu.VMEM((chunks, n_seq * 8, 2 * LANES), f32),
                 pltpu.VMEM((chunks, n_seq * 8, 2 * LANES), f32),
@@ -563,9 +559,9 @@
                 pltpu.VMEM((n_chan, n_seq, MINE, LANES), bf16),
                 pltpu.VMEM((model, LANES), bf16),
                 sems((9,)),
-                sems((4,)),
+                sems((5,)),
             ]
-            + [sems((n_seq,))] * 8
+            + [sems((n_seq,))] * 10
             + [sems, sems, pltpu.SemaphoreType.REGULAR],
             compiler_params=pltpu.CompilerParams(
                 collective_id=0, has_side_effects=True, vmem_limit_bytes=67_043_328

time: 48.8 us -> 47.7 us (0.977)
  Pallas kernels: 44.8 us -> 43.7 us
    pallas_call x1, Pallas kernels: 44.8 us -> 43.7 us  [local(): pl.pallas_call(functools.partial(kernel, n_seq, n_chan), out_shape=(jax.S...]
where the time goes in v6:
time: 47.7 us; the launch traced here: 47.6 us
  Pallas kernels  43.7 us (92%)
  local copies, waits for them, and re-layouts  3.24 us (7%)
  between operations  0.64 us (1%)
    pallas_call x1, Pallas kernels, local(): pl.pallas_call(functools.partial(kernel, n_seq, n_chan), out_shape=(jax.S...  43.7 us
    unnamed x2, local copies, waits for them, and re-layouts  3.24 us

profile of v6, /device:TPU:1, one launch (start us, length us, event | category | flops | bytes accessed | tf_op | source)
XLA Modules:
  0.0 47.6 jit_solution(6164026231867451752)
XLA Ops:
  0.6 43.7 %shard_map.104 = (bf16[64,1024]{1,0:T(8,128)(2,1)}, f32[64,1024]{1,0:T(8,128)}) custom-call(bf16[64,1024]{1,0:T(8,128)(2,1)} %values_hbm.1, bf16[64,1024]{1,0:T(8,128)(2,1)} %gates_hbm.1, bf16[64,1024]{1,0:T(8,128)(2,1)} %cotangent_hbm.1, f32[64,1024]{1,0:T(8,128)} %taps_hbm.1, bf16[4,1024,256]{2,1,0:T(8,128)(2,1)} %constant.6.clone.high_hbm, ...), custom_call_target="tpu_custom_call" | custom-call | tf_op jit(solution)/shard_map/pallas_call | solution.py:516
  44.3 1.6 %copy.13 = bf16[64,1024]{1,0:T(8,128)(2,1)} copy(bf16[64,1024]{1,0:T(8,128)(2,1)} %get-tuple-element.4) | data formatting | bytes 262144
  45.9 1.7 %copy.14 = f32[64,1024]{1,0:T(8,128)} copy(f32[64,1024]{1,0:T(8,128)} %get-tuple-element.5) | data formatting | bytes 524288

commit v7 on v6

--- a/solution.py
+++ b/solution.py
@@ -45,7 +45,7 @@
     wv_hbm,
     wg_hbm,
     input_grad,
-    filter_grad,
+    filter_grad_hbm,
     values,
     gates,
     cotangent,
@@ -82,6 +82,7 @@
     got_f,
     tiles,
     stacked,
+    filter_grad,
     load_sem,
     own_sem,
     u_send,
@@ -124,9 +125,6 @@
             )
         )
     ]
-    for load in loads:
-        load.start()
-
     barrier = pltpu.get_barrier_semaphore()
 
     def greet_seq(k, carry):
@@ -144,6 +142,8 @@
     for k in sorted(range(1, n_seq), key=lambda k: -(k & 2)):
         greet_seq(k, 0)
     lax.fori_loop(1, n_chan, greet_chan, 0)
+    for load in loads:
+        load.start()
 
     for load in loads[:4]:
         load.wait()
@@ -463,6 +463,8 @@
         return carry
 
     lax.fori_loop(0, block // WIDE, join, 0)
+    write_f = pltpu.make_async_copy(filter_grad, filter_grad_hbm, load_sem.at[9])
+    write_f.start()
     loads[7].wait()
     loads[8].wait()
 
@@ -489,6 +491,7 @@
     out = lax.dot_general(tokens[:share], wv[...], turn, preferred_element_type=f32)
     out = out + lax.dot_general(tokens[share:], wg[...], turn, preferred_element_type=f32)
     input_grad[...] = out.astype(bf16)
+    write_f.wait()
 
     def drain(k, carry):
         pltpu.make_async_copy(send_t.at[k], send_t.at[k], t_send).wait()
@@ -520,7 +523,7 @@
                 jax.ShapeDtypeStruct((channels, block), f32),
             ),
             in_specs=[hbm] * 9,
-            out_specs=(vmem, vmem),
+            out_specs=(vmem, hbm),
             scratch_shapes=[
                 pltpu.VMEM((channels, block), bf16),
                 pltpu.VMEM((channels, block), bf16),
@@ -558,7 +561,8 @@
                 pltpu.VMEM((n_seq, block // WIDE, MINE, WIDE), bf16),
                 pltpu.VMEM((n_chan, n_seq, MINE, LANES), bf16),
                 pltpu.VMEM((model, LANES), bf16),
-                sems((9,)),
+                pltpu.VMEM((channels, block), f32),
+                sems((10,)),
                 sems((5,)),
             ]
             + [sems((n_seq,))] * 10

time: 47.7 us -> 47.7 us (level)
  no operation moved by 1% of the time
where the time goes in v7:
time: 47.7 us; the launch traced here: 47.5 us
  Pallas kernels  43.7 us (92%)
  local copies, waits for them, and re-layouts  3.24 us (7%)
  between operations  0.64 us (1%)
    pallas_call x1, Pallas kernels, local(): pl.pallas_call(functools.partial(kernel, n_seq, n_chan), out_shape=(jax.S...  43.7 us
    unnamed x2, local copies, waits for them, and re-layouts  3.24 us

profile of v7, /device:TPU:1, one launch (start us, length us, event | category | flops | bytes accessed | tf_op | source)
XLA Modules:
  0.0 47.5 jit_solution(11347420730590332255)
XLA Ops:
  0.6 43.7 %shard_map.104 = (bf16[64,1024]{1,0:T(8,128)(2,1)}, f32[64,1024]{1,0:T(8,128)}) custom-call(bf16[64,1024]{1,0:T(8,128)(2,1)} %values_hbm.1, bf16[64,1024]{1,0:T(8,128)(2,1)} %gates_hbm.1, bf16[64,1024]{1,0:T(8,128)(2,1)} %cotangent_hbm.1, f32[64,1024]{1,0:T(8,128)} %taps_hbm.1, bf16[4,1024,256]{2,1,0:T(8,128)(2,1)} %constant.6.clone.high_hbm, ...), custom_call_target="tpu_custom_call" | custom-call | tf_op jit(solution)/shard_map/pallas_call | solution.py:519
  44.3 1.6 %copy.13 = bf16[64,1024]{1,0:T(8,128)(2,1)} copy(bf16[64,1024]{1,0:T(8,128)(2,1)} %get-tuple-element.4) | data formatting | bytes 262144
  45.9 1.7 %copy.14 = f32[64,1024]{1,0:T(8,128)} copy(f32[64,1024]{1,0:T(8,128)} %get-tuple-element.5) | data formatting | bytes 524288
